TPU v7x, 32 devices: a whole 2x2x4 slice. The times are simulated.
32 devices in a mesh: dp: 8 (over y, x, core), mp: 4 (over z).
Axes of the slice: x: 2, y: 2, z: 4, core: 2. Of those that a mesh axis runs over, the one named last changes fastest.
Arguments:
- tokens: bfloat16 [24576, 512], P(('dp', 'mp')), may hold values from -6 to 6
- cotangent: bfloat16 [24576, 512], P(('dp', 'mp')), may hold values from -6 to 6
- norm1_gain: float32 [512], replicated, may hold values from 0.4 to 1.6
- norm1_bias: float32 [512], replicated, may hold values from -3 to 3
- query_weight: bfloat16 [512, 512], P(None, 'mp'), may hold values from -0.375 to 0.375
- query_bias: bfloat16 [512], P('mp'), may hold values from -3 to 3
- key_weight: bfloat16 [512, 512], P(None, 'mp'), may hold values from -0.375 to 0.375
- value_weight: bfloat16 [512, 512], P(None, 'mp'), may hold values from -0.25 to 0.25
- value_bias: bfloat16 [512], P('mp'), may hold values from -3 to 3
- out_weight: bfloat16 [512, 512], P('mp'), may hold values from -1 to 1
- out_bias: bfloat16 [512], replicated, may hold values from -3 to 3
- norm2_gain: float32 [512], replicated, may hold values from 0.4 to 1.6
- norm2_bias: float32 [512], replicated, may hold values from -3 to 3
- up_weight: bfloat16 [512, 2048], P(None, 'mp'), may hold values from -0.25 to 0.25
- up_bias: bfloat16 [2048], P('mp'), may hold values from -3 to 3
- down_weight: bfloat16 [2048, 512], P('mp'), may hold values from -0.1875 to 0.1875
- down_bias: bfloat16 [512], replicated, may hold values from -3 to 3
- live_frames: int32 [8], P('dp'), may hold values from 1 to 3, 15 in all
Outputs:
- layer_out: bfloat16 [24576, 512], P(('dp', 'mp'))
- grad_tokens: bfloat16 [24576, 512], P(('dp', 'mp'))
- grad_norm1_gain: float32 [512], replicated
- grad_norm1_bias: float32 [512], replicated
- grad_query_weight: float32 [512, 512], P(None, 'mp')
- grad_query_bias: float32 [512], P('mp')
- grad_key_weight: float32 [512, 512], P(None, 'mp')
- grad_value_weight: float32 [512, 512], P(None, 'mp')
- grad_value_bias: float32 [512], P('mp')
- grad_out_weight: float32 [512, 512], P('mp')
- grad_out_bias: float32 [512], replicated
- grad_norm2_gain: float32 [512], replicated
- grad_norm2_bias: float32 [512], replicated
- grad_up_weight: float32 [512, 2048], P(None, 'mp')
- grad_up_bias: float32 [2048], P('mp')
- grad_down_weight: float32 [2048, 512], P('mp')
- grad_down_bias: float32 [512], replicated
Inputs may be any that keep to these rules, and one draw needn't show every extreme that they name: live_frames[i] counts the frames of the clips assigned to index i of dp; that index's frame slots at or beyond it are padding. Some index is full.
All inputs are finite; a program needn't handle non-finite values. No bound on the sum of `live_frames` on one device may be relied on, other than what follows from the above.
Results may differ from a plain program's by a relative error of at most 0.013.
The roundings to bfloat16 on the way count: a program that leaves them out, or rounds other values in their place, can miss the bound.
Values may be sent and summed in bfloat16 or wider, within the bound.
A program may use at most 128 MiB of HBM per device.

v0:
```python
import jax
import jax.numpy as jnp
from jax import lax
from jax.sharding import PartitionSpec as P

HEAD = 64
PATCH = 1024


EPSILON = 1e-06


def normalize(values, scale_gain, shift_bias):
    center = values - jnp.mean(values, axis=-1, keepdims=True)
    spread = jnp.mean(center * center, axis=-1, keepdims=True)
    return center * lax.rsqrt(spread + EPSILON) * scale_gain + shift_bias


def gelu_tanh(values):
    return jax.nn.gelu(values, approximate=True)


def contract_rows(left_side, right_side):
    return lax.dot_general(
        left_side, right_side, (((0,), (0,)), ((), ())), preferred_element_type=jnp.float32
    )


def times_transposed(left_side, right_side):
    return lax.dot_general(
        left_side, right_side, (((1,), (1,)), ((), ())), preferred_element_type=jnp.float32
    )


def attend_frame(frame_item):
    queries, key_heads, value_heads = frame_item
    scores = jnp.einsum(
        "qhd,khd->hqk", queries, key_heads, preferred_element_type=jnp.float32
    ) * HEAD ** (-0.5)
    row_peak = jnp.max(scores, axis=-1, keepdims=True)
    raised = jnp.exp(scores - row_peak)
    row_total = jnp.sum(raised, axis=-1, keepdims=True)
    softmax_rows = raised / row_total
    mixed_heads = jnp.einsum(
        "hqk,khd->qhd",
        softmax_rows.astype(jnp.bfloat16),
        value_heads,
        preferred_element_type=jnp.float32,
    )
    return (mixed_heads.astype(jnp.bfloat16), row_peak + jnp.log(row_total))


def attend_back(frame_item):
    queries, key_heads, value_heads, grad_mixed, logsum = frame_item
    scale_factor = HEAD ** (-0.5)
    scores = (
        jnp.einsum("qhd,khd->hqk", queries, key_heads, preferred_element_type=jnp.float32)
        * scale_factor
    )
    softmax_rows = jnp.exp(scores - logsum)
    grad_probs = jnp.einsum(
        "qhd,khd->hqk", grad_mixed, value_heads, preferred_element_type=jnp.float32
    )
    center = jnp.sum(softmax_rows * grad_probs, axis=-1, keepdims=True)
    grad_scores = (softmax_rows * (grad_probs - center) * scale_factor).astype(jnp.bfloat16)
    grad_queries = jnp.einsum(
        "hqk,khd->qhd", grad_scores, key_heads, preferred_element_type=jnp.float32
    ).astype(jnp.bfloat16)
    grad_keys = jnp.einsum(
        "hqk,qhd->khd", grad_scores, queries, preferred_element_type=jnp.float32
    ).astype(jnp.bfloat16)
    grad_values = jnp.einsum(
        "hqk,qhd->khd",
        softmax_rows.astype(jnp.bfloat16),
        grad_mixed,
        preferred_element_type=jnp.float32,
    ).astype(jnp.bfloat16)
    return (grad_queries, grad_keys, grad_values)


def per_device(
    tokens,
    cotangent,
    norm1_gain,
    norm1_bias,
    query_weight,
    query_bias,
    key_weight,
    value_weight,
    value_bias,
    out_weight,
    out_bias,
    norm2_gain,
    norm2_bias,
    up_weight,
    up_bias,
    down_weight,
    down_bias,
    live_frames,
):
    local_rows = tokens.shape[0]
    members = lax.axis_size("mp")
    group_rows = local_rows * members
    frames = group_rows // PATCH
    head_cols = query_weight.shape[1]
    heads_here = head_cols // HEAD
    row_index = lax.axis_index("mp") * local_rows + jnp.arange(local_rows, dtype=jnp.int32)
    row_mask = (row_index // PATCH < live_frames[0]).astype(jnp.float32)[:, None]
    inputs = tokens.astype(jnp.float32)
    normed_one, pull_one = jax.vjp(normalize, inputs, norm1_gain, norm1_bias)
    entered_all = lax.all_gather(normed_one.astype(jnp.bfloat16), "mp", axis=0, tiled=True)
    joined_weight = jnp.concatenate((query_weight, key_weight, value_weight), axis=1)
    joined_bias = jnp.concatenate(
        (
            query_bias.astype(jnp.float32),
            jnp.zeros((head_cols,), jnp.float32),
            value_bias.astype(jnp.float32),
        )
    )
    projected = (
        jnp.dot(entered_all, joined_weight, preferred_element_type=jnp.float32) + joined_bias
    ).astype(jnp.bfloat16)
    frame_shape = (frames, PATCH, heads_here, HEAD)
    queries = projected[:, :head_cols].reshape(frame_shape)
    key_heads = projected[:, head_cols : 2 * head_cols].reshape(frame_shape)
    value_heads = projected[:, 2 * head_cols :].reshape(frame_shape)
    mixed_heads, logsum = lax.map(attend_frame, (queries, key_heads, value_heads))
    mixed_heads = mixed_heads.reshape(group_rows, head_cols)
    residual = (
        inputs
        + lax.psum_scatter(
            jnp.dot(mixed_heads, out_weight, preferred_element_type=jnp.float32),
            "mp",
            scatter_dimension=0,
            tiled=True,
        )
        + out_bias.astype(jnp.float32)
    )
    normed_two, pull_two = jax.vjp(normalize, residual, norm2_gain, norm2_bias)
    entered_two = normed_two.astype(jnp.bfloat16)
    entered_two_all = lax.all_gather(entered_two, "mp", axis=0, tiled=True)
    pre_act = jnp.dot(
        entered_two_all, up_weight, preferred_element_type=jnp.float32
    ) + up_bias.astype(jnp.float32)
    activated, pull_act = jax.vjp(gelu_tanh, pre_act)
    activated = activated.astype(jnp.bfloat16)
    feed_out = lax.psum_scatter(
        jnp.dot(activated, down_weight, preferred_element_type=jnp.float32).astype(jnp.bfloat16),
        "mp",
        scatter_dimension=0,
        tiled=True,
    ).astype(jnp.float32) + down_bias.astype(jnp.float32)
    layer_out = (row_mask * (residual + feed_out)).astype(jnp.bfloat16)
    grad_layer = row_mask * cotangent.astype(jnp.float32)
    grad_feed = grad_layer.astype(jnp.bfloat16)
    grad_down_bias = jnp.sum(grad_feed.astype(jnp.float32), axis=0)
    grad_feed_all = lax.all_gather(grad_feed, "mp", axis=0, tiled=True)
    grad_pre = pull_act(times_transposed(grad_feed_all, down_weight))[0].astype(jnp.bfloat16)
    grad_down = contract_rows(activated, grad_feed_all)
    grad_up = contract_rows(entered_two_all, grad_pre)
    grad_up_bias = jnp.sum(grad_pre.astype(jnp.float32), axis=0)
    grad_normed_two = lax.psum_scatter(
        times_transposed(grad_pre, up_weight), "mp", scatter_dimension=0, tiled=True
    )
    grad_from_norm, grad_norm2_gain, grad_norm2_bias = pull_two(grad_normed_two)
    grad_residual = grad_layer + grad_from_norm
    grad_attended = grad_residual.astype(jnp.bfloat16)
    grad_out_bias = jnp.sum(grad_attended.astype(jnp.float32), axis=0)
    grad_attended_all = lax.all_gather(grad_attended, "mp", axis=0, tiled=True)
    grad_mixed = times_transposed(grad_attended_all, out_weight).astype(jnp.bfloat16)
    grad_out = contract_rows(mixed_heads, grad_attended_all)
    grad_queries, grad_keys, grad_values = lax.map(
        attend_back, (queries, key_heads, value_heads, grad_mixed.reshape(frame_shape), logsum)
    )
    grad_projected = jnp.concatenate(
        (
            grad_queries.reshape(group_rows, head_cols),
            grad_keys.reshape(group_rows, head_cols),
            grad_values.reshape(group_rows, head_cols),
        ),
        axis=1,
    )
    grad_joined = contract_rows(entered_all, grad_projected)
    grad_joined_bias = jnp.sum(grad_projected.astype(jnp.float32), axis=0)
    grad_normed_one = lax.psum_scatter(
        times_transposed(grad_projected, joined_weight), "mp", scatter_dimension=0, tiled=True
    )
    grad_inputs, grad_norm1_gain, grad_norm1_bias = pull_one(grad_normed_one)
    grad_tokens = (grad_residual + grad_inputs).astype(jnp.bfloat16)
    grad_joined, grad_out, grad_up, grad_down, grad_joined_bias, grad_up_bias = lax.psum(
        (grad_joined, grad_out, grad_up, grad_down, grad_joined_bias, grad_up_bias), "dp"
    )
    small_sums = lax.psum(
        (
            grad_norm1_gain,
            grad_norm1_bias,
            grad_norm2_gain,
            grad_norm2_bias,
            grad_out_bias,
            grad_down_bias,
        ),
        ("dp", "mp"),
    )
    return (
        layer_out,
        grad_tokens,
        small_sums[0],
        small_sums[1],
        grad_joined[:, :head_cols],
        grad_joined_bias[:head_cols],
        grad_joined[:, head_cols : 2 * head_cols],
        grad_joined[:, 2 * head_cols :],
        grad_joined_bias[2 * head_cols :],
        grad_out,
        small_sums[4],
        small_sums[2],
        small_sums[3],
        grad_up,
        grad_up_bias,
        grad_down,
        small_sums[5],
    )


def solution(mesh):
    in_specs = (
        P(("dp", "mp"), None),
        P(("dp", "mp"), None),
        P(),
        P(),
        P(None, "mp"),
        P("mp"),
        P(None, "mp"),
        P(None, "mp"),
        P("mp"),
        P("mp", None),
        P(),
        P(),
        P(),
        P(None, "mp"),
        P("mp"),
        P("mp", None),
        P(),
        P("dp"),
    )
    out_specs = (
        P(("dp", "mp"), None),
        P(("dp", "mp"), None),
        P(),
        P(),
        P(None, "mp"),
        P("mp"),
        P(None, "mp"),
        P(None, "mp"),
        P("mp"),
        P("mp", None),
        P(),
        P(),
        P(),
        P(None, "mp"),
        P("mp"),
        P("mp", None),
        P(),
    )
    return jax.shard_map(
        per_device, mesh=mesh, in_specs=in_specs, out_specs=out_specs, check_vma=False
    )
```

profile of v0, /device:TPU:1, one launch (start us, length us, event | category | flops | bytes accessed | tf_op | source)
XLA Modules:
  0.0 1010.3 jit_solution(15482708863742551023)
XLA Ops:
  7.3 1.5 convert_reduce_fusion.2
  8.8 1.5 fusion.107
  10.3 2.4 fusion.105
  13.0 65.4 %all-gather.5.cloned.1.call-done = bf16[3072,512]{1,0:T(8,128)(2,1)} async-done(((bf16[768,512]{1,0:T(8,128)(2,1)}), bf16[3072,512]{1,0:T(8,128)(2,1)}) %all-gather.5.cloned.1.call-update) | async-done | bytes 3145744 | tf_op jit(solution)/shard_map/all_gather | solution.py:111
  78.4 3.7 add_convert_fusion
  82.1 1.5 fusion.127
  85.5 4.0 reshape.181
  89.5 3.5 copy.54
  93.0 1.6 reshape.180
  94.6 3.5 copy.53
  99.1 17.4 %while.26 = (s32[]{:T(128)}, bf16[3,1024,2,64]{1,3,2,0:T(8,128)(2,1)}, f32[3,2,1024,1]{2,1,3,0:T(2,128)}, bf16[3,1024,2,64]{1,3,2,0:T(8,128)(2,1)S(1)}, bf16[3,1...) while((s32[]{:T(128)}, bf16[3,1024,2,64]{1,3,2,0:T(8,128)(2,1)}, ...), condition=%wide.region_5.6_spmd, body=%wide.region_2.5_spmd.sunk | while | flops 555874304 | bytes 26282072 | solution.py:127
  100.4 1.4 fusion.181
  101.8 2.5 fusion.182
  107.6 2.5 fusion.182
  113.4 2.5 fusion.182
  116.5 2.4 copy.56
  120.1 3.7 fusion.130
  124.5 109.0 %reduce-scatter.5.cloned.1.call-done = f32[768,512]{1,0:T(8,128)} async-done(((f32[3072,512]{1,0:T(8,128)}), f32[768,512]{1,0:T(8,128)}) %reduce-scatter.5.cloned.1.call-update) | async-done | bytes 1572880 | tf_op jit(solution)/shard_map/reduce_scatter | solution.py:131
  233.5 1.7 fusion.125
  235.6 1.9 add_convert_fusion.2
  238.3 2.8 convert_reduce_fusion.3
  242.4 59.2 %all-gather.7.cloned.1.call-done = bf16[3072,512]{1,0:T(8,128)(2,1)} async-done(((bf16[768,512]{1,0:T(8,128)(2,1)}), bf16[3072,512]{1,0:T(8,128)(2,1)}) %all-gather.7.cloned.1.call-update) | async-done | bytes 3145744 | tf_op jit(solution)/shard_map/all_gather | solution.py:141
  301.6 6.3 fusion.131
  307.9 57.8 %all-gather.9.cloned.1.call-done = bf16[3072,512]{1,0:T(8,128)(2,1)} async-done(((bf16[768,512]{1,0:T(8,128)(2,1)}), bf16[3072,512]{1,0:T(8,128)(2,1)}) %all-gather.9.cloned.1.call-update) | async-done | bytes 3145744 | tf_op jit(solution)/shard_map/all_gather | solution.py:157
  365.8 10.3 %convert_reduce_fusion = (f32[512]{0:T(512)}, bf16[3072,512]{1,0:T(8,128)(2,1)S(1)}, bf16[3072,512]{1,0:T(8,128)(2,1)}) fusion(f32[3072,512]{1,0:T(8,128)} %fusion.131, f32[512]{0:T(512)} %convert_element_type.117, bf16[3072,512]{1,0:T(8,128)(2,1)} %all-gather.9.cloned.1.call-done, bf16[512,512]{1,0:T(8,128)(2,1)S(1)} %copy-done), kind=kOutput, calls=%fused_computation.77 | convolution fusion | flops 1649933824 | bytes 16257024 | tf_op jit(solution)/shard_map/dot_general | solution.py:30
  376.1 1.7 copy-done.17
  377.8 4.6 fusion.132
  382.5 5.4 convolution_convert_fusion
  388.5 103.5 %reduce-scatter.9.cloned.1.call-done = f32[768,512]{1,0:T(8,128)} async-done(((f32[3072,512]{1,0:T(8,128)}), f32[768,512]{1,0:T(8,128)}) %reduce-scatter.9.cloned.1.call-update) | async-done | bytes 1572880 | tf_op jit(solution)/shard_map/reduce_scatter | solution.py:162
  492.0 2.0 multiply_reduce_fusion.2
  494.1 60.7 %reduce-scatter.7.cloned.1.call-done = bf16[768,512]{1,0:T(8,128)(2,1)} async-done(((bf16[3072,512]{1,0:T(8,128)(2,1)}), bf16[768,512]{1,0:T(8,128)(2,1)}) %reduce-scatter.7.cloned.1.call-update) | async-done | bytes 786448 | tf_op jit(solution)/shard_map/reduce_scatter | solution.py:147
  554.8 3.0 fusion.124
  560.5 5.8 fusion.137
  566.3 2.8 fusion.136
  569.1 55.0 %all-gather.11.cloned.1.call-done = bf16[3072,512]{1,0:T(8,128)(2,1)} async-done(((bf16[768,512]{1,0:T(8,128)(2,1)}), bf16[3072,512]{1,0:T(8,128)(2,1)}) %all-gather.11.cloned.1.call-update) | async-done | bytes 3145744 | tf_op jit(solution)/shard_map/all_gather | solution.py:169
  624.0 3.7 convolution_convert_fusion.1
  627.8 4.0 reshape.179
  631.8 4.7 copy.60
  639.5 120.6 %while.27 = (s32[]{:T(128)}, bf16[3,1024,2,64]{1,3,2,0:T(8,128)(2,1)}, bf16[3,1024,2,64]{1,3,2,0:T(8,128)(2,1)}, bf16[3,1024,2,64]{1,3,2,0:T(8,128)(2,1)}, bf16[...) while((s32[]{:T(128)}, ...), condition=%wide.region_15.16_spmd, body=%wide.region_13.15_spmd.sunk | while | flops 1386616832 | bytes 131658920 | solution.py:172
  641.6 2.9 fusion.197
  644.9 5.5 fusion.193
  650.4 13.7 %fusion.196 = bf16[3,1024,2,64]{1,3,2,0:T(8,128)(2,1)} fusion(bf16[3,1024,2,64]{1,3,2,0:T(8,128)(2,1)} %get-tuple-element.334, s32[]{:T(128)S(6)} %copy.101, f32[2,1024,1024]{1,2,0:T(8,128)} %fusion.193, f32[2,1024,1024]{1,2,0:T(8,128)} %copy-done.2, f32[2,1024]{1,0:T(2,128)S(1)} %dynamic-slice_bitcast_fusion.2, ...), kind=kOutput, calls=%fused_computation.38.clone.1 | convolution fusion | flops 287443968 | bytes 34096128 | tf_op jit(solution)/shard_map/while/body/eval_jaxpr/hqk,qhd->khd/dot_general | solution.py:69
  664.1 15.6 %fusion.195 = bf16[3,1024,2,64]{1,3,2,0:T(8,128)(2,1)} fusion(bf16[3,1024,2,64]{1,3,2,0:T(8,128)(2,1)} %get-tuple-element.333, s32[]{:T(128)S(6)} %copy.101, f32[2,1024,1024]{1,2,0:T(8,128)} %fusion.193, f32[2,1024,1024]{1,2,0:T(8,128)} %copy-done.2, f32[2,1024]{1,0:T(2,128)S(1)} %dynamic-slice_bitcast_fusion.2, ...), kind=kOutput, calls=%fused_computation.40.clone.1 | convolution fusion | flops 287443968 | bytes 34096128 | tf_op jit(solution)/shard_map/while/body/eval_jaxpr/hqk,khd->qhd/dot_general | solution.py:66
  681.7 2.9 fusion.197
  685.0 5.5 fusion.193
  690.5 13.7 %fusion.196 = bf16[3,1024,2,64]{1,3,2,0:T(8,128)(2,1)} fusion(bf16[3,1024,2,64]{1,3,2,0:T(8,128)(2,1)} %get-tuple-element.334, s32[]{:T(128)S(6)} %copy.101, f32[2,1024,1024]{1,2,0:T(8,128)} %fusion.193, f32[2,1024,1024]{1,2,0:T(8,128)} %copy-done.2, f32[2,1024]{1,0:T(2,128)S(1)} %dynamic-slice_bitcast_fusion.2, ...), kind=kOutput, calls=%fused_computation.38.clone.1 | convolution fusion | flops 287443968 | bytes 34096128 | tf_op jit(solution)/shard_map/while/body/eval_jaxpr/hqk,qhd->khd/dot_general | solution.py:69
  704.2 15.6 %fusion.195 = bf16[3,1024,2,64]{1,3,2,0:T(8,128)(2,1)} fusion(bf16[3,1024,2,64]{1,3,2,0:T(8,128)(2,1)} %get-tuple-element.333, s32[]{:T(128)S(6)} %copy.101, f32[2,1024,1024]{1,2,0:T(8,128)} %fusion.193, f32[2,1024,1024]{1,2,0:T(8,128)} %copy-done.2, f32[2,1024]{1,0:T(2,128)S(1)} %dynamic-slice_bitcast_fusion.2, ...), kind=kOutput, calls=%fused_computation.40.clone.1 | convolution fusion | flops 287443968 | bytes 34096128 | tf_op jit(solution)/shard_map/while/body/eval_jaxpr/hqk,khd->qhd/dot_general | solution.py:66
  721.8 2.9 fusion.197
  725.2 5.5 fusion.193
  730.6 13.7 %fusion.196 = bf16[3,1024,2,64]{1,3,2,0:T(8,128)(2,1)} fusion(bf16[3,1024,2,64]{1,3,2,0:T(8,128)(2,1)} %get-tuple-element.334, s32[]{:T(128)S(6)} %copy.101, f32[2,1024,1024]{1,2,0:T(8,128)} %fusion.193, f32[2,1024,1024]{1,2,0:T(8,128)} %copy-done.2, f32[2,1024]{1,0:T(2,128)S(1)} %dynamic-slice_bitcast_fusion.2, ...), kind=kOutput, calls=%fused_computation.38.clone.1 | convolution fusion | flops 287443968 | bytes 34096128 | tf_op jit(solution)/shard_map/while/body/eval_jaxpr/hqk,qhd->khd/dot_general | solution.py:69
  744.3 15.6 %fusion.195 = bf16[3,1024,2,64]{1,3,2,0:T(8,128)(2,1)} fusion(bf16[3,1024,2,64]{1,3,2,0:T(8,128)(2,1)} %get-tuple-element.333, s32[]{:T(128)S(6)} %copy.101, f32[2,1024,1024]{1,2,0:T(8,128)} %fusion.193, f32[2,1024,1024]{1,2,0:T(8,128)} %copy-done.2, f32[2,1024]{1,0:T(2,128)S(1)} %dynamic-slice_bitcast_fusion.2, ...), kind=kOutput, calls=%fused_computation.40.clone.1 | convolution fusion | flops 287443968 | bytes 34096128 | tf_op jit(solution)/shard_map/while/body/eval_jaxpr/hqk,khd->qhd/dot_general | solution.py:66
  760.2 1.9 copy.64
  766.3 1.5 fusion.135
  767.8 2.7 fusion.134
  771.5 6.2 fusion.133
  777.7 2.1 convert_reduce_fusion.1
  779.8 13.0 %all-reduce.1 = (f32[384]{0:T(512)S(1)}, f32[512]{0:T(512)}) all-reduce(f32[384]{0:T(512)S(1)} %convert_reduce_fusion.1, f32[512]{0:T(512)S(1)} %copy-done.42), channel_id=1, replica_groups=mesh['dp'=8,'mp'=4] {'dp'}, use_global_device_ids=true, to_apply=%region_25.26 | all-reduce | flops 896 | bytes 7168 | tf_op jit(solution)/shard_map/psum | solution.py:190
  793.3 46.2 %all-reduce.5.cloned.1.call-done = (f32[512,384]{1,0:T(8,128)}, f32[128,512]{1,0:T(8,128)}, f32[512,512]{1,0:T(8,128)}, f32[512,512]{1,0:T(8,128)}) async-done(((f32[512,384]{1,0:T(8,128)}, f32[128,512]{1,0:T(8,128)}, f32[512,512]{1,0:T(8,128)}, f32[512,512]{1,0:T(8,128)}), (f32[512,384]{1,0:T(8,128)}, f32[128,512]{1,0:T(8,128)}, f32[512,512]{1,0:T(8,128)}, ...) | async-done | bytes 3145744 | tf_op jit(solution)/shard_map/psum | solution.py:190
  839.5 2.0 fusion.128
  841.5 111.4 %reduce-scatter.11.cloned.1.call-done = f32[768,512]{1,0:T(8,128)} async-done(((f32[3072,512]{1,0:T(8,128)}), f32[768,512]{1,0:T(8,128)}) %reduce-scatter.11.cloned.1.call-update) | async-done | bytes 1572880 | tf_op jit(solution)/shard_map/reduce_scatter | solution.py:185
  953.0 2.0 fusion.120
  955.8 40.5 %all-reduce = (f32[512]{0:T(512)}, f32[512]{0:T(512)}, f32[512]{0:T(512)}, f32[512]{0:T(512)}, f32[512]{0:T(512)}, /*index=5*/f32[512]{0:T(512)}) all-reduce(f32[512]{0:T(512)S(1)} %get-tuple-element.136, f32[512]{0:T(512)S(1)} %get-tuple-element.139, f32[512]{0:T(512)S(1)} %get-tuple-element.187, ...), channel_id=1, replica_groups=mesh['dp'=8,'mp'=4] {'dp','mp'}, use_global_device_ids=true, to_apply=%region_20.21 | all-reduce | flops 3072 | bytes 24576 | tf_op jit(solution)/shard_map/psum | solution.py:193
  996.3 3.1 add_convert_fusion.1
  1000.1 2.3 copy.119
  (176 shorter events, 37.1 us)
Async XLA Ops:
  7.2 358.6 %copy-start = (bf16[512,512]{1,0:T(8,128)(2,1)S(1)}, bf16[512,512]{1,0:T(8,128)(2,1)}, u32[]{:S(2)}) copy-start(bf16[512,512]{1,0:T(8,128)(2,1)} %param.37) | copy-start | bytes 1572868
  7.2 5.6 copy-start.46
  7.2 5.6 copy-start.47
  7.2 5.6 copy-start.31
  7.2 5.7 copy-start.32
  7.2 5.7 copy-start.33
  7.3 71.2 %all-gather.5.cloned.1.call-start = ((), (), s32[]{:S(2)}) async-start(), calls=%async_computation.4 | async-start | bytes 3932160 | tf_op jit(solution)/shard_map/all_gather | solution.py:111
  8.8 4.1 copy-start.29
  10.3 2.6 copy-start.36
  10.3 2.6 copy-start.34
  12.7 220.8 %reduce-scatter.5.cloned.1.call-start = ((), (), s32[]{:S(2)}) async-start(), calls=%async_computation.5 | async-start | bytes 7864320 | tf_op jit(solution)/shard_map/reduce_scatter | solution.py:131
  13.0 65.4 %copy-start.25 = (bf16[512,384]{1,0:T(8,128)(2,1)}, bf16[512,384]{1,0:T(8,128)(2,1)S(1)}, u32[]{:S(2)}) copy-start(bf16[512,384]{1,0:T(8,128)(2,1)S(1)} %constant_dynamic-update-slice_fusion) | copy-start | bytes 1179652
  85.5 7.5 copy-start.20
  116.5 7.3 copy-start.6
  116.5 7.3 copy-start.8
  116.5 7.3 copy-start.16
  116.5 3.7 copy-start.27
  119.3 0.9 copy-start.13
  123.8 0.7 copy-start.43
  123.8 109.7 %copy-start.3 = (bf16[768,512]{1,0:T(8,128)(2,1)S(1)}, bf16[768,512]{1,0:T(8,128)(2,1)}, u32[]{:S(2)}) copy-start(bf16[768,512]{1,0:T(8,128)(2,1)} %param.22) | copy-start | bytes 2359300
  123.9 111.7 %copy-start.39 = (f32[512]{0:T(512)S(1)}, f32[512]{0:T(512)}, u32[]{:S(2)}) copy-start(f32[512]{0:T(512)} %param.33) | copy-start | bytes 6148
  123.9 177.7 %all-gather.7.cloned.1.call-start = ((), (), s32[]{:S(2)}) async-start(), calls=%async_computation.6 | async-start | bytes 3932160 | tf_op jit(solution)/shard_map/all_gather | solution.py:141
  235.6 66.1 %copy-start.23 = (bf16[512,512]{1,0:T(8,128)(2,1)S(1)}, bf16[512,512]{1,0:T(8,128)(2,1)}, u32[]{:S(2)}) copy-start(bf16[512,512]{1,0:T(8,128)(2,1)} %param.35) | copy-start | bytes 1572868
  237.5 128.3 %all-gather.9.cloned.1.call-start = ((), (), s32[]{:S(2)}) async-start(), calls=%async_computation.8 | async-start | bytes 3932160 | tf_op jit(solution)/shard_map/all_gather | solution.py:157
  241.1 250.9 %reduce-scatter.9.cloned.1.call-start = ((), (), s32[]{:S(2)}) async-start(), calls=%async_computation.9 | async-start | bytes 7864320 | tf_op jit(solution)/shard_map/reduce_scatter | solution.py:162
  376.1 1.7 copy-start.17
  382.4 172.4 %reduce-scatter.7.cloned.1.call-start = ((), (), s32[]{:S(2)}) async-start(), calls=%async_computation.7 | async-start | bytes 3932160 | tf_op jit(solution)/shard_map/reduce_scatter | solution.py:147
  387.8 0.7 copy-start.44
  387.8 104.2 %copy-start.40 = (f32[512]{0:T(512)S(1)}, f32[512]{0:T(512)}, u32[]{:S(2)}) copy-start(f32[512]{0:T(512)} %param.33) | copy-start | bytes 6148
  387.8 236.2 %all-gather.11.cloned.1.call-start = ((), (), s32[]{:S(2)}) async-start(), calls=%async_computation.10 | async-start | bytes 3932160 | tf_op jit(solution)/shard_map/all_gather | solution.py:169
  554.8 4.2 copy-start.15
  557.8 1.2 copy-start.12
  560.2 279.3 %all-reduce.5.cloned.1.call-start = ((), (), s32[]{:S(2)}) async-start(), calls=%async_computation.12 | async-start | bytes 6291456 | tf_op jit(solution)/shard_map/psum | solution.py:190
  560.5 5.8 copy-start.18
  560.5 5.8 copy-start.19
  627.8 11.8 %copy-start.7 = (bf16[3,1024,2,64]{1,3,2,0:T(8,128)(2,1)S(1)}, bf16[3,1024,2,64]{1,3,2,0:T(8,128)(2,1)}, u32[]{:S(2)}) copy-start(bf16[3,1024,2,64]{1,3,2,0:T(8,128)(2,1)} %copy-done.6) | copy-start | bytes 2359300
  627.8 11.8 %copy-start.9 = (bf16[3,1024,2,64]{1,3,2,0:T(8,128)(2,1)S(1)}, bf16[3,1024,2,64]{1,3,2,0:T(8,128)(2,1)}, u32[]{:S(2)}) copy-start(bf16[3,1024,2,64]{1,3,2,0:T(8,128)(2,1)} %copy-done.8) | copy-start | bytes 2359300
  640.2 1.3 copy-start.10
  641.5 3.3 copy-start.2
  680.4 1.3 copy-start.10
  681.7 3.3 copy-start.2
  720.5 1.3 copy-start.10
  721.8 3.3 copy-start.2
  760.2 2.3 copy-start.22
  762.1 1.4 copy-start.21
  764.2 1.9 copy-start.4
  764.2 2.1 copy-start.14
  764.7 3.1 copy-start.45
  766.3 1.5 copy-start.5
  770.5 1.0 copy-start.26
  770.5 182.4 %reduce-scatter.11.cloned.1.call-start = ((), (), s32[]{:S(2)}) async-start(), calls=%async_computation.11 | async-start | bytes 7864320 | tf_op jit(solution)/shard_map/reduce_scatter | solution.py:185
  777.6 2.1 copy-start.42
  777.7 175.3 %copy-start.30 = (f32[768]{0:T(1024)S(1)}, f32[768]{0:T(1024)}, u32[]{:S(2)}) copy-start(f32[768]{0:T(1024)} %copy-done.29) | copy-start | bytes 9220
  777.7 175.3 %copy-start.38 = (f32[512]{0:T(512)S(1)}, f32[512]{0:T(512)}, u32[]{:S(2)}) copy-start(f32[512]{0:T(512)} %param.24) | copy-start | bytes 6148
  777.7 177.3 %copy-start.37 = (f32[768]{0:T(1024)S(1)}, f32[768]{0:T(1024)}, u32[]{:S(2)}) copy-start(f32[768]{0:T(1024)} %copy-done.36) | copy-start | bytes 9220
  777.7 177.3 %copy-start.35 = (f32[768]{0:T(1024)S(1)}, f32[768]{0:T(1024)}, u32[]{:S(2)}) copy-start(f32[768]{0:T(1024)} %copy-done.34) | copy-start | bytes 9220
  839.5 116.3 %copy-start.41 = (f32[512]{0:T(512)S(1)}, f32[512]{0:T(512)}, u32[]{:S(2)}) copy-start(f32[512]{0:T(512)} %get-tuple-element.185) | copy-start | bytes 6148
  952.9 2.0 copy-start.11
  955.8 43.6 %copy-start.28 = (f32[128,512]{1,0:T(8,128)S(1)}, f32[128,512]{1,0:T(8,128)}, u32[]{:S(2)}) copy-start(f32[128,512]{1,0:T(8,128)} %get-tuple-element.361) | copy-start | bytes 786436
  996.3 6.0 copy-start.24
  996.3 7.0 copy-start.1
Sparse Core Ops, SparseCore 0:
  12.8 65.5 all-gather.4
  124.0 109.5 reduce-scatter.4
  237.7 63.9 all-gather.6
  303.6 62.1 all-gather.8
  382.5 109.4 reduce-scatter.8
  494.2 60.5 reduce-scatter.6
  560.3 63.6 all-gather.10
  770.6 68.8 all-reduce.4
  841.9 110.9 reduce-scatter.10
where the time goes:
time: 1020 us; the launch traced here: 1010 us
  waiting for transfers between devices  668 us (65%)
  matrix products  185 us (18%)
  blocking collectives  53.5 us (5%)
  local copies, waits for them, and re-layouts  53.3 us (5%)
  other arithmetic  33.6 us (3%)
  between operations  15.6 us (2%)
    reduce_scatter x1, waiting for transfers between devices, per_device(): lax.psum_scatter(times_transposed(grad_projected, joined_weight), 'mp', s...  111 us
    reduce_scatter x1, waiting for transfers between devices, per_device(): lax.psum_scatter(jnp.dot(mixed_heads, out_weight, preferred_element_type=...  109 us
    reduce_scatter x1, waiting for transfers between devices, per_device(): lax.psum_scatter(times_transposed(grad_pre, up_weight), 'mp', scatter_dim...  104 us
    all_gather x1, waiting for transfers between devices, per_device(): lax.all_gather(normed_one.astype(jnp.bfloat16), 'mp', axis=0, tiled=True)  65.4 us
    reduce_scatter x1, waiting for transfers between devices, per_device(): lax.psum_scatter(jnp.dot(activated, down_weight, preferred_element_type=j...  60.7 us
    all_gather x1, waiting for transfers between devices, per_device(): entered_two_all = lax.all_gather(entered_two, 'mp', axis=0, tiled=True)  59.2 us
    all_gather x1, waiting for transfers between devices, per_device(): grad_feed_all = lax.all_gather(grad_feed, 'mp', axis=0, tiled=True)  57.8 us
    all_gather x1, waiting for transfers between devices, per_device(): grad_attended_all = lax.all_gather(grad_attended, 'mp', axis=0, tiled=True)  55 us
  transfers between devices with their start and end apart: 9, of which 9 were waited for; matrix products, arithmetic and copies ran while one was open for 4% of the time, Pallas kernels for 0%

commit v1 on v0

v1 whole, which is shorter than its diff:
```python
import functools

import jax
import jax.numpy as jnp
from jax import lax
from jax.experimental import pallas as pl
from jax.experimental.pallas import tpu as pltpu
from jax.sharding import PartitionSpec as P

HEAD = 64
PATCH = 1024
PAIR = 2 * HEAD
EPSILON = 1e-06
MESH = pl.DeviceIdType.MESH
BF16 = jnp.bfloat16
F32 = jnp.float32
GELU_C = 0.7978845608028654
GELU_A = 0.044715

SEGMENTS = (
    ((0, 768, 0, 0, 1),),
    ((0, 256, 0, 768, 0), (256, 512, 1, 0, 2)),
    ((0, 512, 1, 512, 1), (512, 256, 0, 0, 3)),
    ((0, 768, 0, 256, 2),),
)
TASKS = (
    ((0, 0), (0, 1), (0, 2)),
    ((0, 3), (1, 0), (1, 1)),
    ((0, 0), (1, 2), (1, 3)),
    ((0, 1), (0, 2), (0, 3)),
)
ANY = pl.BlockSpec(memory_space=pl.ANY)


def partner_segment(me, slot):
    other = [seg[4] for seg in SEGMENTS[me] if seg[2] == slot][0]
    return other, [seg for seg in SEGMENTS[other] if seg[4] == me and seg[2] == slot][0]


def nt_dot(a, b):
    return lax.dot_general(a, b, (((1,), (1,)), ((), ())), preferred_element_type=F32)


def tn_dot(a, b):
    return lax.dot_general(a, b, (((0,), (0,)), ((), ())), preferred_element_type=F32)


def nn_dot(a, b):
    return jnp.dot(a, b, preferred_element_type=F32)


def place():
    d, m = lax.axis_index("dp"), lax.axis_index("mp")
    core, b1, b2 = d % 2, (d // 2) % 2, (d // 4) % 2
    lo = b1 + core * (b2 - b1)
    hi = b2 + core * (b1 - b2)
    flip_lo = d + (1 - core) * (2 - 4 * b1) + core * (4 - 8 * b2)
    flip_hi = d + (1 - core) * (4 - 8 * b2) + core * (2 - 4 * b1)
    flip_core = d + 1 - 2 * core
    return d, m, core, lo, hi, flip_lo, flip_hi, flip_core


def barrier(targets):
    sem = pltpu.get_barrier_semaphore()
    for dev in targets:
        pl.semaphore_signal(sem, inc=1, device_id=dev, device_id_type=MESH)
    pl.semaphore_wait(sem, len(targets))


def neighbour_barrier(d, m):
    sem = pltpu.get_barrier_semaphore()
    for k in range(4):
        @pl.when(m == k)
        def _():
            others = sorted({seg[4] for seg in SEGMENTS[k]})
            for o in others:
                pl.semaphore_signal(sem, inc=1, device_id=(d, o), device_id_type=MESH)
            pl.semaphore_wait(sem, len(others))


def gather_kernel(x_ref, wq_ref, wr_ref, bias_ref, t_ref, gq_ref, gr_ref, gb_ref,
                  local, zsend, zrecv, psend, precv, tsend, trecv, bsend, brecv):
    d, m, core, lo, hi, flip_lo, flip_hi, flip_core = place()
    others = [(m + j) % 4 for j in (1, 2, 3)]
    barrier([(d, o) for o in others] + [(flip_lo, m), (flip_hi, m), (flip_core, m)])
    rq, rr = wq_ref.shape[0] // 8, wr_ref.shape[0] // 8
    piece = 4 * core + 2 * hi + lo
    sent = []

    def push(src, dst, ssem, rsem, dev):
        c = pltpu.make_async_remote_copy(src, dst, ssem, rsem, device_id=dev, device_id_type=MESH)
        c.start()
        sent.append(c)
        return c

    zq, zr = [], []
    for j in range(3):
        dev = (d, others[j])
        sl = pl.ds(pl.multiple_of(piece * rq, 16), rq)
        zq.append(push(wq_ref.at[sl, :], gq_ref.at[m, sl, :], zsend.at[0, j], zrecv.at[0, j], dev))
    for j in range(3):
        push(bias_ref, gb_ref.at[m], bsend.at[j], brecv.at[j], (d, others[j]))
    for k in range(4):
        @pl.when(m == k)
        def _():
            for i, (ls, n, slot, fs, other) in enumerate(SEGMENTS[k]):
                pltpu.make_async_remote_copy(
                    x_ref.at[pl.ds(ls, n), :], t_ref.at[slot, pl.ds(fs, n), :],
                    tsend.at[i], trecv.at[slot], device_id=(d, other), device_id_type=MESH).start()
    for j in range(3):
        dev = (d, others[j])
        sl = pl.ds(pl.multiple_of(piece * rr, 16), rr)
        zr.append(push(wr_ref.at[sl, :], gr_ref.at[m, sl, :], zsend.at[1, j], zrecv.at[1, j], dev))
    own = [
        pltpu.make_async_copy(wq_ref, gq_ref.at[m], local.at[0]),
        pltpu.make_async_copy(wr_ref, gr_ref.at[m], local.at[1]),
        pltpu.make_async_copy(bias_ref, gb_ref.at[m], local.at[2]),
    ]
    for c in own:
        c.start()
    for k in range(4):
        @pl.when(m == k)
        def _():
            cs = [pltpu.make_async_copy(x_ref.at[pl.ds(ls, n), :], t_ref.at[slot, pl.ds(fs, n), :],
                                        local.at[3 + i])
                  for i, (ls, n, slot, fs, other) in enumerate(SEGMENTS[k])]
            for c in cs:
                c.start()
            for c in cs:
                c.wait()
    froms = [(m + 3 - j) % 4 for j in range(3)]
    stages = ((flip_lo, piece, 1), (flip_hi, 4 * core + 2 * hi, 2), (flip_core, 4 * core, 4))
    prev = [zq, zr]
    for st, (dev, first, count) in enumerate(stages):
        cur = [[], []]
        for a, (g_ref, rows) in enumerate(((gq_ref, rq), (gr_ref, rr))):
            for j in range(3):
                prev[a][j].wait_recv()
                sl = pl.ds(pl.multiple_of(first * rows, 16), count * rows)
                part = g_ref.at[froms[j], sl, :]
                cur[a].append(push(part, part, psend.at[st, a, j], precv.at[st, a, j], (dev, m)))
        prev = cur
    for a in range(2):
        for j in range(3):
            prev[a][j].wait_recv()
    for j in range(3):
        pltpu.make_async_remote_copy(bias_ref, gb_ref.at[m], bsend.at[j], brecv.at[j],
                                     device_id=(d, others[j]), device_id_type=MESH).wait_recv()
    for c in own:
        c.wait()
    for c in sent:
        c.wait_send()
    for j in range(3):
        pass
    for k in range(4):
        @pl.when(m == k)
        def _():
            for i, (ls, n, slot, fs, other) in enumerate(SEGMENTS[k]):
                _, (pls, pn, _, pfs, _) = partner_segment(k, slot)
                pltpu.make_async_remote_copy(
                    x_ref.at[pl.ds(ls, n), :], t_ref.at[slot, pl.ds(fs, n), :],
                    tsend.at[i], trecv.at[slot], device_id=(d, other), device_id_type=MESH).wait_send()
                pltpu.make_async_remote_copy(
                    x_ref.at[pl.ds(0, pn), :], t_ref.at[slot, pl.ds(pfs, pn), :],
                    tsend.at[i], trecv.at[slot], device_id=(d, other), device_id_type=MESH).wait_recv()


def gather(x, wq, wr, bias):
    dma = pltpu.SemaphoreType.DMA
    return pl.pallas_call(
        gather_kernel,
        name="gather",
        out_shape=(
            jax.ShapeDtypeStruct((2, PATCH, x.shape[1]), BF16),
            jax.ShapeDtypeStruct((4,) + wq.shape, BF16),
            jax.ShapeDtypeStruct((4,) + wr.shape, BF16),
            jax.ShapeDtypeStruct((4,) + bias.shape, F32),
        ),
        in_specs=[ANY] * 4,
        out_specs=(ANY,) * 4,
        scratch_shapes=[dma((5,)), dma((2, 3)), dma((2, 3)), dma((3, 2, 3)), dma((3, 2, 3)),
                        dma((2,)), dma((2,)), dma((3,)), dma((3,))],
        compiler_params=pltpu.CompilerParams(collective_id=0, has_side_effects=True),
    )(x, wq, wr, bias)


def attend_kernel(slot_ref, shard_ref, t_ref, w_ref, b_ref, g1_ref, e_ref, qkv_ref, p_ref, l_ref, ot_ref, o_ref,
                  kt_sc):
    x = t_ref[0].astype(F32)
    mean = jnp.mean(x, axis=-1, keepdims=True)
    cen = x - mean
    var = jnp.mean(cen * cen, axis=-1, keepdims=True)
    ent = (cen * lax.rsqrt(var + EPSILON) * g1_ref[0:1, :] + g1_ref[1:2, :]).astype(BF16)
    e_ref[0] = ent
    bias = b_ref[0, 0:1, :]
    q = (nn_dot(ent, w_ref[0, :, 0:PAIR]) + bias[:, 0:PAIR]).astype(BF16)
    k = nn_dot(ent, w_ref[0, :, PAIR:2 * PAIR]).astype(BF16)
    v = (nn_dot(ent, w_ref[0, :, 2 * PAIR:]) + bias[:, PAIR:2 * PAIR]).astype(BF16)
    qs = q * jnp.asarray(HEAD ** -0.5, BF16)
    qkv_ref[0, :, 0:PAIR] = qs
    qkv_ref[0, :, PAIR:2 * PAIR] = k
    qkv_ref[0, :, 2 * PAIR:] = v
    qt = qs.astype(F32).T.astype(BF16)
    vt = v.astype(F32).T.astype(BF16)
    lane = lax.broadcasted_iota(jnp.int32, (1, PAIR), 1)
    width = 256
    for h in range(2):
        kt_sc[h] = jnp.where((lane // HEAD) == h, k, jnp.zeros_like(k))
    for c in range(PATCH // width):
        cols = slice(c * width, (c + 1) * width)
        outs = []
        for h in range(2):
            st = nn_dot(kt_sc[h], qt[:, cols])
            peak = jnp.max(st, axis=0, keepdims=True)
            raised = jnp.exp(st - peak)
            total = jnp.sum(raised, axis=0, keepdims=True)
            pb = raised.astype(BF16)
            p_ref[0, h, :, cols] = pb
            inv = 1.0 / total
            l_ref[0, h:h + 1, cols] = inv
            outs.append(nn_dot(vt[h * HEAD:(h + 1) * HEAD], pb) * inv)
        ot = jnp.concatenate(outs, axis=0)
        ot_ref[0, :, cols] = ot
        o_ref[0, cols, :] = ot.T.astype(BF16)


def attend(slots, shards, tokens2, gq, gb, g1):
    return pl.pallas_call(
        attend_kernel,
        name="attend",
        grid_spec=pltpu.PrefetchScalarGridSpec(
            num_scalar_prefetch=2,
            grid=(3,),
            in_specs=[
                pl.BlockSpec((1, PATCH, 512), lambda t, sl, sh: (sl[t], 0, 0)),
                pl.BlockSpec((1, 512, 384), lambda t, sl, sh: (sh[t], 0, 0)),
                pl.BlockSpec((1, 8, 768), lambda t, sl, sh: (sh[t], 0, 0)),
                pl.BlockSpec((8, 512), lambda t, sl, sh: (0, 0)),
            ],
            out_specs=[
                pl.BlockSpec((1, PATCH, 512), lambda t, sl, sh: (t, 0, 0)),
                pl.BlockSpec((1, PATCH, 384), lambda t, sl, sh: (t, 0, 0)),
                pl.BlockSpec((1, 2, PATCH, PATCH), lambda t, sl, sh: (t, 0, 0, 0)),
                pl.BlockSpec((1, 8, PATCH), lambda t, sl, sh: (t, 0, 0)),
                pl.BlockSpec((1, PAIR, PATCH), lambda t, sl, sh: (t, 0, 0)),
                pl.BlockSpec((1, PATCH, PAIR), lambda t, sl, sh: (t, 0, 0)),
            ],
            scratch_shapes=[pltpu.VMEM((2, PATCH, PAIR), BF16)],
        ),
        out_shape=[
            jax.ShapeDtypeStruct((3, PATCH, 512), BF16),
            jax.ShapeDtypeStruct((3, PATCH, 384), BF16),
            jax.ShapeDtypeStruct((3, 2, PATCH, PATCH), BF16),
            jax.ShapeDtypeStruct((3, 8, PATCH), F32),
            jax.ShapeDtypeStruct((3, PAIR, PATCH), F32),
            jax.ShapeDtypeStruct((3, PATCH, PAIR), BF16),
        ],
        compiler_params=pltpu.CompilerParams(vmem_limit_bytes=60 << 20),
    )(slots, shards, tokens2, gq, gb, g1)


def heads_out_kernel(o_ref, mix_ref, local, send, recv):
    d, m = lax.axis_index("dp"), lax.axis_index("mp")
    neighbour_barrier(d, m)
    for k in range(4):
        @pl.when(m == k)
        def _():
            copies, remote, arrive = [], [], []
            for t, (slot, pair) in enumerate(TASKS[k]):
                cols = pl.ds(pair * PAIR, PAIR)
                other, (pls, pn, _, pfs, _) = partner_segment(k, slot)
                c = pltpu.make_async_remote_copy(
                    o_ref.at[t, pl.ds(pfs, pn), :], mix_ref.at[pl.ds(pls, pn), cols],
                    send.at[t], recv.at[slot, pair], device_id=(d, other), device_id_type=MESH)
                c.start()
                remote.append(c)
                ls, n, _, fs, _ = [seg for seg in SEGMENTS[k] if seg[2] == slot][0]
                c = pltpu.make_async_copy(o_ref.at[t, pl.ds(fs, n), :], mix_ref.at[pl.ds(ls, n), cols],
                                          local.at[t])
                c.start()
                copies.append(c)
            for ls, n, slot, fs, other in SEGMENTS[k]:
                for slot2, pair in TASKS[other]:
                    if slot2 == slot:
                        part = mix_ref.at[pl.ds(ls, n), pl.ds(pair * PAIR, PAIR)]
                        arrive.append(pltpu.make_async_remote_copy(
                            part, part, send.at[0], recv.at[slot, pair],
                            device_id=(d, other), device_id_type=MESH))
            for c in copies:
                c.wait()
            for c in remote:
                c.wait_send()
            for c in arrive:
                c.wait_recv()


def heads_out(o, rows):
    dma = pltpu.SemaphoreType.DMA
    return pl.pallas_call(
        heads_out_kernel,
        name="heads_out",
        out_shape=jax.ShapeDtypeStruct((rows, 4 * PAIR), BF16),
        in_specs=[ANY],
        out_specs=ANY,
        scratch_shapes=[dma((3,)), dma((3,)), dma((2, 4))],
        compiler_params=pltpu.CompilerParams(collective_id=1, has_side_effects=True),
    )(o)


def heads_in_kernel(do_ref, task_ref, local, send, recv):
    d, m = lax.axis_index("dp"), lax.axis_index("mp")
    neighbour_barrier(d, m)
    for k in range(4):
        @pl.when(m == k)
        def _():
            copies, remote, arrive = [], [], []
            n_sent = 0
            for ls, n, slot, fs, other in SEGMENTS[k]:
                for t, (slot2, pair) in enumerate(TASKS[other]):
                    if slot2 == slot:
                        c = pltpu.make_async_remote_copy(
                            do_ref.at[pl.ds(ls, n), pl.ds(pair * PAIR, PAIR)], task_ref.at[t, pl.ds(fs, n), :],
                            send.at[n_sent], recv.at[t], device_id=(d, other), device_id_type=MESH)
                        c.start()
                        n_sent += 1
                        remote.append(c)
            for t, (slot, pair) in enumerate(TASKS[k]):
                ls, n, _, fs, _ = [seg for seg in SEGMENTS[k] if seg[2] == slot][0]
                c = pltpu.make_async_copy(do_ref.at[pl.ds(ls, n), pl.ds(pair * PAIR, PAIR)],
                                          task_ref.at[t, pl.ds(fs, n), :], local.at[t])
                c.start()
                copies.append(c)
                other, (pls, pn, _, pfs, _) = partner_segment(k, slot)
                part = task_ref.at[t, pl.ds(pfs, pn), :]
                arrive.append(pltpu.make_async_remote_copy(
                    part, part, send.at[0], recv.at[t], device_id=(d, other), device_id_type=MESH))
            for c in copies:
                c.wait()
            for c in remote:
                c.wait_send()
            for c in arrive:
                c.wait_recv()


def heads_in(do):
    dma = pltpu.SemaphoreType.DMA
    return pl.pallas_call(
        heads_in_kernel,
        name="heads_in",
        out_shape=jax.ShapeDtypeStruct((3, PATCH, PAIR), BF16),
        in_specs=[ANY],
        out_specs=ANY,
        scratch_shapes=[dma((3,)), dma((5,)), dma((3,))],
        compiler_params=pltpu.CompilerParams(collective_id=2, has_side_effects=True),
    )(do)


def rows_back_kernel(pn_ref, own_ref, got_ref, local, send, recv):
    d, m = lax.axis_index("dp"), lax.axis_index("mp")
    neighbour_barrier(d, m)
    for k in range(4):
        @pl.when(m == k)
        def _():
            copies, remote, arrive = [], [], []
            for i, (ls, n, slot, fs, other) in enumerate(SEGMENTS[k]):
                _, (pls, pn, _, pfs, _) = partner_segment(k, slot)
                c = pltpu.make_async_remote_copy(
                    pn_ref.at[slot, pl.ds(pfs, pn), :], got_ref.at[pl.ds(pls, pn), :],
                    send.at[i], recv.at[slot], device_id=(d, other), device_id_type=MESH)
                c.start()
                remote.append(c)
                c = pltpu.make_async_copy(pn_ref.at[slot, pl.ds(fs, n), :], own_ref.at[pl.ds(ls, n), :],
                                          local.at[i])
                c.start()
                copies.append(c)
                part = got_ref.at[pl.ds(ls, n), :]
                arrive.append(pltpu.make_async_remote_copy(
                    part, part, send.at[i], recv.at[slot], device_id=(d, other), device_id_type=MESH))
            for c in copies:
                c.wait()
            for c in remote:
                c.wait_send()
            for c in arrive:
                c.wait_recv()


def rows_back(pn, rows):
    dma = pltpu.SemaphoreType.DMA
    return pl.pallas_call(
        rows_back_kernel,
        name="rows_back",
        out_shape=(jax.ShapeDtypeStruct((rows, 512), BF16),) * 2,
        in_specs=[ANY],
        out_specs=(ANY, ANY),
        scratch_shapes=[dma((2,)), dma((2,)), dma((2,))],
        compiler_params=pltpu.CompilerParams(collective_id=3, has_side_effects=True),
    )(pn)


def middle_kernel(x_ref, cot_ref, mask_ref, mix_ref, wr_ref, gb_ref, vec_ref,
                  out_ref, gres_ref, do_ref, gr_ref, small_ref,
                  wo_sc, e2t_sc, e2_sc, gf_sc, res_sc, xhat_sc, feed_sc, gn_sc, rstd_sc):
    rows = x_ref.shape[0]
    for s in range(4):
        wo_sc[s * PAIR:(s + 1) * PAIR, :] = wr_ref[s, 0:PAIR, :]
    res = x_ref[...].astype(F32) + nn_dot(mix_ref[...], wo_sc[...]) + vec_ref[0:1, :]
    mean = jnp.mean(res, axis=-1, keepdims=True)
    cen = res - mean
    var = jnp.mean(cen * cen, axis=-1, keepdims=True)
    rstd = lax.rsqrt(var + EPSILON)
    xhat = cen * rstd
    e2f = xhat * vec_ref[1:2, :] + vec_ref[2:3, :]
    e2 = e2f.astype(BF16)
    e2_sc[...] = e2
    e2t_sc[...] = e2.astype(F32).T.astype(BF16)
    res_sc[...] = res
    xhat_sc[...] = xhat
    rstd_sc[...] = jnp.broadcast_to(rstd, rstd_sc.shape)
    gl = mask_ref[...] * cot_ref[...].astype(F32)
    gf = gl.astype(BF16)
    gf_sc[...] = gf
    small_ref[5:6, :] = jnp.sum(gf.astype(F32), axis=0, keepdims=True)
    feed_sc[...] = jnp.zeros_like(feed_sc)
    gn_sc[...] = jnp.zeros_like(gn_sc)

    def hidden(s, carry):
        up = wr_ref[s, PAIR:PAIR + 512, :]
        down = wr_ref[s, PAIR + 512:, :]
        pre = nn_dot(e2_sc[...], up) + gb_ref[s, 0:1, 256:768]
        sq = pre * pre
        th = jnp.tanh(GELU_C * pre * (1.0 + GELU_A * sq))
        half = 0.5 * (1.0 + th)
        act = (pre * half).astype(BF16)
        slope = half + (0.5 * GELU_C) * pre * (1.0 - th * th) * (1.0 + (3.0 * GELU_A) * sq)
        gp = (slope * nt_dot(gf_sc[...], down)).astype(BF16)
        feed_sc[...] += nn_dot(act, down)
        gn_sc[...] += nt_dot(gp, up)
        gr_ref[s, PAIR:PAIR + 512, :] = nn_dot(e2t_sc[...], gp).astype(BF16)
        gr_ref[s, PAIR + 512:, :] = tn_dot(act, gf_sc[...]).astype(BF16)
        small_ref[pl.ds(8 + s, 1), :] = jnp.sum(gp.astype(F32), axis=0, keepdims=True)
        return carry

    lax.fori_loop(0, 4, hidden, 0)
    out_ref[...] = (mask_ref[...] * (res_sc[...] + feed_sc[...] + vec_ref[3:4, :])).astype(BF16)
    gn = gn_sc[...]
    xhat = xhat_sc[...]
    small_ref[2:3, :] = jnp.sum(gn * xhat, axis=0, keepdims=True)
    small_ref[3:4, :] = jnp.sum(gn, axis=0, keepdims=True)
    gg = gn * vec_ref[1:2, :]
    mg = jnp.mean(gg, axis=-1, keepdims=True)
    mx = jnp.mean(gg * xhat, axis=-1, keepdims=True)
    gres = mask_ref[...] * cot_ref[...].astype(F32) + rstd_sc[:, 0:1] * (gg - mg - xhat * mx)
    gres_ref[...] = gres
    ga = gres.astype(BF16)
    small_ref[4:5, :] = jnp.sum(ga.astype(F32), axis=0, keepdims=True)
    gw = tn_dot(mix_ref[...], ga).astype(BF16)
    for s in range(4):
        gr_ref[s, 0:PAIR, :] = gw[s * PAIR:(s + 1) * PAIR, :]
    do_ref[...] = nt_dot(ga, wo_sc[...]).astype(BF16)


def middle(x, cot, mask, mix, gr, gb, vec):
    rows = x.shape[0]
    return pl.pallas_call(
        middle_kernel,
        name="middle",
        out_shape=(
            jax.ShapeDtypeStruct((rows, 512), BF16),
            jax.ShapeDtypeStruct((rows, 512), F32),
            jax.ShapeDtypeStruct((rows, 512), BF16),
            jax.ShapeDtypeStruct(gr.shape, BF16),
            jax.ShapeDtypeStruct((16, 512), F32),
        ),
        scratch_shapes=[
            pltpu.VMEM((512, 512), BF16),
            pltpu.VMEM((512, rows), BF16),
            pltpu.VMEM((rows, 512), BF16),
            pltpu.VMEM((rows, 512), BF16),
            pltpu.VMEM((rows, 512), F32),
            pltpu.VMEM((rows, 512), F32),
            pltpu.VMEM((rows, 512), F32),
            pltpu.VMEM((rows, 512), F32),
            pltpu.VMEM((rows, 128), F32),
        ],
        compiler_params=pltpu.CompilerParams(vmem_limit_bytes=60 << 20),
    )(x, cot, mask, mix, gr, gb, vec)


def attend_back_kernel(slot_ref, shard_ref, do_ref, qkv_ref, p_ref, l_ref, ot_ref, e_ref, w_ref,
                       gq_ref, pn_ref, bias_ref, ds_sc, dot_sc, dom_sc, dkv_sc):
    t = pl.program_id(0)

    @pl.when(t == 3)
    def _():
        gq_ref[...] = jnp.zeros_like(gq_ref)
        bias_ref[...] = jnp.zeros_like(bias_ref)

    @pl.when(t < 3)
    def _():
        lane = lax.broadcasted_iota(jnp.int32, (1, PAIR), 1)
        dot_full = do_ref[0].astype(F32).T
        inv = l_ref[0]
        scaled = jnp.concatenate([dot_full[0:HEAD] * inv[0:1, :], dot_full[HEAD:] * inv[1:2, :]], axis=0)
        dot_sc[...] = scaled.astype(BF16)
        dop = dot_sc[...].astype(F32).T.astype(BF16)
        qs = qkv_ref[0, :, 0:PAIR]
        k = qkv_ref[0, :, PAIR:2 * PAIR]
        v = qkv_ref[0, :, 2 * PAIR:]
        kt = k.astype(F32).T.astype(BF16)
        zero = jnp.zeros_like(k)
        width = 256
        prod = dot_sc[...].astype(F32) * ot_ref[0]
        dqt = []
        for h in range(2):
            sel = (lane // HEAD) == h
            center = jnp.sum(prod[h * HEAD:(h + 1) * HEAD], axis=0, keepdims=True)
            vm = jnp.where(sel, v, zero)
            for c in range(PATCH // width):
                cols = slice(c * width, (c + 1) * width)
                dpt = nn_dot(vm, dot_sc[:, cols])
                ds_sc[:, cols] = (p_ref[0, h, :, cols].astype(F32) * (dpt - center[:, cols])).astype(BF16)
            dqt.append(nn_dot(kt[h * HEAD:(h + 1) * HEAD], ds_sc[...]))
            dk = nn_dot(ds_sc[...], jnp.where(sel, qs, zero))
            dv = nn_dot(p_ref[0, h], jnp.where(sel, dop, zero))
            if h == 0:
                dkv_sc[0] = dk
                dkv_sc[1] = dv
            else:
                dk = dkv_sc[0] + dk
                dv = dkv_sc[1] + dv
        dq = (jnp.concatenate(dqt, axis=0) * HEAD ** -0.5).T
        dqkv = jnp.concatenate([dq.astype(BF16), dk.astype(BF16), dv.astype(BF16)], axis=1)
        bias_ref[0] = jnp.broadcast_to(jnp.sum(dqkv.astype(F32), axis=0, keepdims=True), bias_ref.shape[1:])
        gq_ref[0] = tn_dot(e_ref[0], dqkv).astype(BF16)
        back = nt_dot(dqkv, w_ref[0])
        first = jnp.logical_or(t == 0, slot_ref[t] != slot_ref[jnp.maximum(t - 1, 0)])

        @pl.when(first)
        def _():
            pn_ref[0] = back

        @pl.when(jnp.logical_not(first))
        def _():
            pn_ref[0] += back


def attend_back(slots, shards, do, qkv, p, linv, ot, ent, gq):
    def task(t):
        return jnp.minimum(t, 2)

    return pl.pallas_call(
        attend_back_kernel,
        name="attend_back",
        grid_spec=pltpu.PrefetchScalarGridSpec(
            num_scalar_prefetch=2,
            grid=(4,),
            in_specs=[
                pl.BlockSpec((1, PATCH, PAIR), lambda t, sl, sh: (task(t), 0, 0)),
                pl.BlockSpec((1, PATCH, 384), lambda t, sl, sh: (task(t), 0, 0)),
                pl.BlockSpec((1, 2, PATCH, PATCH), lambda t, sl, sh: (task(t), 0, 0, 0)),
                pl.BlockSpec((1, 8, PATCH), lambda t, sl, sh: (task(t), 0, 0)),
                pl.BlockSpec((1, PAIR, PATCH), lambda t, sl, sh: (task(t), 0, 0)),
                pl.BlockSpec((1, PATCH, 512), lambda t, sl, sh: (task(t), 0, 0)),
                pl.BlockSpec((1, 512, 384), lambda t, sl, sh: (sh[task(t)], 0, 0)),
            ],
            out_specs=[
                pl.BlockSpec((1, 512, 384), lambda t, sl, sh: (sh[t], 0, 0)),
                pl.BlockSpec((1, PATCH, 512), lambda t, sl, sh: (sl[task(t)], 0, 0)),
                pl.BlockSpec((1, 8, 384), lambda t, sl, sh: (sh[t], 0, 0)),
            ],
            scratch_shapes=[
                pltpu.VMEM((PATCH, PATCH), BF16),
                pltpu.VMEM((PAIR, PATCH), BF16),
                pltpu.VMEM((2, PATCH, PAIR), BF16),
                pltpu.VMEM((2, PATCH, PAIR), F32),
            ],
        ),
        out_shape=[
            jax.ShapeDtypeStruct((4, 512, 384), BF16),
            jax.ShapeDtypeStruct((2, PATCH, 512), F32),
            jax.ShapeDtypeStruct((4, 8, 384), F32),
        ],
        compiler_params=pltpu.CompilerParams(vmem_limit_bytes=60 << 20),
    )(slots, shards, do, qkv, p, linv, ot, ent, gq)


def first_back_kernel(x_ref, gres_ref, own_ref, got_ref, vec_ref, gt_ref, small_ref):
    x = x_ref[...].astype(F32)
    mean = jnp.mean(x, axis=-1, keepdims=True)
    cen = x - mean
    var = jnp.mean(cen * cen, axis=-1, keepdims=True)
    rstd = lax.rsqrt(var + EPSILON)
    xhat = cen * rstd
    gn = own_ref[...].astype(F32) + got_ref[...].astype(F32)
    small_ref[...] = jnp.zeros_like(small_ref)
    small_ref[0:1, :] = jnp.sum(gn * xhat, axis=0, keepdims=True)
    small_ref[1:2, :] = jnp.sum(gn, axis=0, keepdims=True)
    gg = gn * vec_ref[0:1, :]
    mg = jnp.mean(gg, axis=-1, keepdims=True)
    mx = jnp.mean(gg * xhat, axis=-1, keepdims=True)
    gt_ref[...] = (gres_ref[...] + rstd * (gg - mg - xhat * mx)).astype(BF16)


def first_back(x, gres, own, got, vec):
    return pl.pallas_call(
        first_back_kernel,
        name="first_back",
        out_shape=(jax.ShapeDtypeStruct(x.shape, BF16), jax.ShapeDtypeStruct((8, 512), F32)),
        compiler_params=pltpu.CompilerParams(vmem_limit_bytes=60 << 20),
    )(x, gres, own, got, vec)


def reduce_kernel(n_high, q_ref, r_ref, s_ref, oq_ref, or_ref, os_ref,
                  q3, r3, q2, r2, q1, r1, qz, rz, qh, rh, sm, send, recv):
    d, m, core, lo, hi, flip_lo, flip_hi, flip_core = place()
    others = [(m + j) % 4 for j in (1, 2, 3)]
    highs = []
    for b in range(n_high):
        step = 8 * 2 ** b
        bit = (d // step) % 2
        highs.append(d + step - 2 * step * bit)
    barrier([(d, o) for o in others] + [(flip_lo, m), (flip_hi, m), (flip_core, m)] + [(h, m) for h in highs])
    rq, rr = q_ref.shape[1] // 8, r_ref.shape[1] // 8
    sent = []
    count = [0]

    def push(src, dst, dev):
        i = count[0]
        count[0] += 1
        c = pltpu.make_async_remote_copy(src, dst, send.at[i], recv.at[i], device_id=dev, device_id_type=MESH)
        c.start()
        sent.append(c)
        return c

    def rows(first, n, size):
        return pl.ds(pl.multiple_of(first * size, 16), n * size)

    stages = (
        (flip_core, 4 * (1 - core), 4 * core, 4, q3, r3),
        (flip_hi, 4 * core + 2 * (1 - hi), 4 * core + 2 * hi, 2, q2, r2),
        (flip_lo, 4 * core + 2 * hi + 1 - lo, 4 * core + 2 * hi + lo, 1, q1, r1),
    )
    os_ref[...] = s_ref[...]
    for st, (dev, away, mine, n, qb, rb) in enumerate(stages):
        sm[2 * st] = os_ref[...]
        cr = push(r_ref.at[:, rows(away, n, rr), :], rb, (dev, m))
        cq = push(q_ref.at[:, rows(away, n, rq), :], qb, (dev, m))
        cs = push(sm.at[2 * st], sm.at[2 * st + 1], (dev, m))
        for c, ref, buf, size in ((cr, r_ref, rb, rr), (cq, q_ref, qb, rq)):
            c.wait_recv()

            def add(s, carry, ref=ref, buf=buf, size=size):
                sl = rows(mine, n, size)
                ref[s, sl, :] = (ref[s, sl, :].astype(F32) + buf[s].astype(F32)).astype(BF16)
                return carry

            lax.fori_loop(0, 4, add, 0)
        cs.wait_recv()
        os_ref[...] += sm[2 * st + 1]
    piece = 4 * core + 2 * hi + lo
    sm[6] = os_ref[...]
    arrive = []
    for j in range(3):
        dev = (d, others[j])
        arrive.append((
            push(r_ref.at[others[j], rows(piece, 1, rr), :], rz.at[j], dev),
            push(q_ref.at[others[j], rows(piece, 1, rq), :], qz.at[j], dev),
            push(sm.at[6], sm.at[7 + j], dev),
        ))
    acc_r = r_ref[m, rows(piece, 1, rr), :].astype(F32)
    acc_q = q_ref[m, rows(piece, 1, rq), :].astype(F32)
    acc_s = os_ref[...]
    for j in range(3):
        for c in arrive[j]:
            c.wait_recv()
        acc_r += rz[j].astype(F32)
        acc_q += qz[j].astype(F32)
        acc_s += sm[7 + j]
    for b in range(n_high):
        rh[2 * b] = acc_r.astype(BF16)
        qh[2 * b] = acc_q.astype(BF16)
        sm[10 + 2 * b] = acc_s
        cs = (
            push(rh.at[2 * b], rh.at[2 * b + 1], (highs[b], m)),
            push(qh.at[2 * b], qh.at[2 * b + 1], (highs[b], m)),
            push(sm.at[10 + 2 * b], sm.at[11 + 2 * b], (highs[b], m)),
        )
        for c in cs:
            c.wait_recv()
        acc_r += rh[2 * b + 1].astype(F32)
        acc_q += qh[2 * b + 1].astype(F32)
        acc_s += sm[11 + 2 * b]
    os_ref[...] = acc_s
    or_ref[rows(piece, 1, rr), :] = acc_r.astype(BF16)
    oq_ref[rows(piece, 1, rq), :] = acc_q.astype(BF16)
    for dev, first, n in ((flip_lo, piece, 1), (flip_hi, 4 * core + 2 * hi, 2), (flip_core, 4 * core, 4)):
        a = or_ref.at[rows(first, n, rr), :]
        b = oq_ref.at[rows(first, n, rq), :]
        ca = push(a, a, (dev, m))
        cb = push(b, b, (dev, m))
        ca.wait_recv()
        cb.wait_recv()
    for c in sent:
        c.wait_send()


def reduce_gradients(n_high, gq, gr, small):
    dma = pltpu.SemaphoreType.DMA
    rq, rr = gq.shape[1] // 8, gr.shape[1] // 8
    cq, cr = gq.shape[2], gr.shape[2]
    vmem = pl.BlockSpec(memory_space=pltpu.VMEM)
    copies = 9 + 9 + 3 * n_high + 6
    scratch = []
    for n in (4, 2, 1):
        scratch += [pltpu.VMEM((4, n * rq, cq), BF16), pltpu.VMEM((4, n * rr, cr), BF16)]
    scratch += [pltpu.VMEM((3, rq, cq), BF16), pltpu.VMEM((3, rr, cr), BF16)]
    scratch += [pltpu.VMEM((max(2 * n_high, 1), rq, cq), BF16), pltpu.VMEM((max(2 * n_high, 1), rr, cr), BF16)]
    scratch += [pltpu.VMEM((10 + 2 * n_high,) + small.shape, F32), dma((copies,)), dma((copies,))]
    return pl.pallas_call(
        functools.partial(reduce_kernel, n_high),
        name="reduce",
        out_shape=(
            jax.ShapeDtypeStruct((8 * rq, cq), BF16),
            jax.ShapeDtypeStruct((8 * rr, cr), BF16),
            jax.ShapeDtypeStruct(small.shape, F32),
        ),
        in_specs=[vmem] * 3,
        out_specs=(vmem,) * 3,
        scratch_shapes=scratch,
        input_output_aliases={},
        compiler_params=pltpu.CompilerParams(collective_id=4, has_side_effects=True, vmem_limit_bytes=60 << 20),
    )(gq, gr, small)


def per_device(n_high, tokens, cotangent, norm1_gain, norm1_bias, query_weight, query_bias, key_weight,
               value_weight, value_bias, out_weight, out_bias, norm2_gain, norm2_bias, up_weight, up_bias,
               down_weight, down_bias, live_frames):
    rows = tokens.shape[0]
    m = lax.axis_index("mp")
    row_index = m * rows + jnp.arange(rows, dtype=jnp.int32)
    mask = (row_index // PATCH < live_frames[0]).astype(F32)[:, None]
    wq = jnp.concatenate((query_weight, key_weight, value_weight), axis=1)
    wr = jnp.concatenate((out_weight, up_weight, down_weight), axis=0)
    bias = jnp.broadcast_to(
        jnp.concatenate((query_bias, value_bias, up_bias)).astype(F32)[None, :], (8, 768))
    g1 = jnp.stack([norm1_gain, norm1_bias] * 4)
    zero = jnp.zeros((512,), F32)
    vec = jnp.stack([out_bias.astype(F32), norm2_gain, norm2_bias, down_bias.astype(F32),
                     zero, zero, zero, zero])
    slots = jnp.asarray([[t[0] for t in ts] for ts in TASKS], jnp.int32)[m]
    shards = jnp.asarray([[t[1] for t in ts] + [3 - i] for i, ts in enumerate(TASKS)], jnp.int32)
    missing = jnp.asarray([6 - sum(t[1] for t in ts) for ts in TASKS], jnp.int32)
    shards = shards[m].at[3].set(missing[m])
    t2, gq, gr, gb = gather(tokens, wq, wr, bias)
    ent, qkv, p, linv, ot, o = attend(slots, shards, t2, gq, gb, g1)
    mix = heads_out(o, rows)
    layer_out, gres, do, dr, small = middle(tokens, cotangent, mask, mix, gr, gb, vec)
    dot = heads_in(do)
    dq, pn, dbias = attend_back(slots, shards, dot, qkv, p, linv, ot, ent, gq)
    own, got = rows_back(pn.astype(BF16), rows)
    grad_tokens, small1 = first_back(tokens, gres, own, got, g1)
    rows_small = jnp.concatenate(
        (small1[0:2], small[2:12], jnp.pad(dbias[:, 0, :], ((0, 0), (0, 128)))), axis=0)
    fq, fr, fs = reduce_gradients(n_high, dq, dr, rows_small)
    fq = fq.astype(F32)
    fr = fr.astype(F32)
    gu = lax.dynamic_slice_in_dim(fs, 8 + m, 1, 0)[0]
    gqb = lax.dynamic_slice_in_dim(fs, 12 + m, 1, 0)[0]
    return (
        layer_out,
        grad_tokens,
        fs[0],
        fs[1],
        fq[:, :PAIR],
        gqb[:PAIR],
        fq[:, PAIR:2 * PAIR],
        fq[:, 2 * PAIR:],
        gqb[2 * PAIR:3 * PAIR],
        fr[0:PAIR],
        fs[4],
        fs[2],
        fs[3],
        fr[PAIR:PAIR + 512],
        gu,
        fr[PAIR + 512:],
        fs[5],
    )


def solution(mesh):
    rows, reps, cols = P(("dp", "mp"), None), P(), P(None, "mp")
    part, split = P("mp"), P("mp", None)
    in_specs = (rows, rows, reps, reps, cols, part, cols, cols, part, split, reps, reps, reps, cols, part,
                split, reps, P("dp"))
    out_specs = (rows, rows, reps, reps, cols, part, cols, cols, part, split, reps, reps, reps, cols, part,
                 split, reps)
    n_high = (mesh.shape["dp"] // 8).bit_length() - 1
    return jax.shard_map(
        functools.partial(per_device, n_high), mesh=mesh, in_specs=in_specs, out_specs=out_specs,
        check_vma=False,
    )
```

time: 1020 us -> 341 us (0.33)
  waiting for transfers between devices: 668 us -> 0 us
  Pallas kernels: 0 us -> 314 us
  matrix products: 185 us -> 0 us
  blocking collectives: 53.5 us -> 0 us
  local copies, waits for them, and re-layouts: 53.3 us -> 13.7 us
  other arithmetic: 33.6 us -> 8.61 us
  between operations: 15.6 us -> 1.54 us
    reduce_scatter x4 -> x0, waiting for transfers between devices: 385 us -> none  [the longest x1 111 us: per_device(): lax.psum_scatter(times_transposed(grad_projected, joined_weight), 'mp', s...]
    pallas_call x0 -> x9, Pallas kernels: none -> 314 us  [the longest x1 103 us: gather(): pl.pallas_call(gather_kernel, name='gather', out_shape=(jax.ShapeDtypeStr...]
    all_gather x4 -> x0, waiting for transfers between devices: 237 us -> none  [the longest x1 65.4 us: per_device(): lax.all_gather(normed_one.astype(jnp.bfloat16), 'mp', axis=0, tiled=True)]
    dot_general x33 -> x0, matrix products: 185 us -> none  [the longest x3 46.9 us: attend_back(): jnp.einsum('hqk,khd->qhd', grad_scores, key_heads, preferred_element_type...]
    psum x2 -> x0, blocking collectives: 53.5 us -> none  [the longest x1 40.5 us: per_device(): lax.psum((grad_norm1_gain, grad_norm1_bias, grad_norm2_gain, grad_norm2_b...]
    psum x1 -> x0, waiting for transfers between devices: 46.2 us -> none  [per_device(): lax.psum((grad_joined, grad_out, grad_up, grad_down, grad_joined_bias, gr...]
    reduce_sum x14 -> x0, other arithmetic: 23 us -> none  [the longest x3 6.14 us: normalize(): center = values - jnp.mean(values, axis=-1, keepdims=True)]
    while x20 -> x0, local copies, waits for them, and re-layouts: 19.8 us -> none  [the longest x4 10.5 us: per_device(): lax.map(attend_frame, (queries, key_heads, value_heads))]
  transfers between devices with their start and end apart: 9 -> 0, of which waited for: 9 -> 0; matrix products, arithmetic and copies ran while one was open for 4% -> 0% of each run, Pallas kernels for 0% -> 0%
where the time goes in v1:
time: 341 us; the launch traced here: 338 us
  Pallas kernels  314 us (92%)
  local copies, waits for them, and re-layouts  13.7 us (4%)
  other arithmetic  8.61 us (3%)
    pallas_call x1, Pallas kernels, gather(): pl.pallas_call(gather_kernel, name='gather', out_shape=(jax.ShapeDtypeStr...  103 us
    pallas_call x1, Pallas kernels, reduce_gradients(): pl.pallas_call(functools.partial(reduce_kernel, n_high), name='reduce', o...  74.1 us
    pallas_call x1, Pallas kernels, attend(): pl.pallas_call(attend_kernel, name='attend', grid_spec=pltpu.PrefetchScal...  26.2 us
    pallas_call x1, Pallas kernels, rows_back(): pl.pallas_call(rows_back_kernel, name='rows_back', out_shape=(jax.ShapeDt...  25 us
    pallas_call x1, Pallas kernels, attend_back(): pl.pallas_call(attend_back_kernel, name='attend_back', grid_spec=pltpu.Pr...  22.4 us
    pallas_call x1, Pallas kernels, middle(): pl.pallas_call(middle_kernel, name='middle', out_shape=(jax.ShapeDtypeStr...  21 us
    pallas_call x1, Pallas kernels, heads_out(): pl.pallas_call(heads_out_kernel, name='heads_out', out_shape=jax.ShapeDty...  19.4 us
    pallas_call x1, Pallas kernels, heads_in(): pl.pallas_call(heads_in_kernel, name='heads_in', out_shape=jax.ShapeDtype...  19.1 us

profile of v1, /device:TPU:1, one launch (start us, length us, event | category | flops | bytes accessed | tf_op | source)
XLA Modules:
  0.0 337.9 jit_solution(15466187609616472466)
XLA Ops:
  0.7 0.0 copy-start.3
  0.7 0.0 copy-start.2
  0.7 0.0 copy-start.1
  0.7 0.0 copy-start.15
  0.7 0.0 copy-start.14
  0.7 0.0 copy-start.13
  0.7 0.8 fusion.6
  1.5 0.8 constant_dynamic-update-slice_fusion.shard_ref
  2.3 0.0 copy-start.8
  2.3 1.2 fusion.5.slot_ref
  3.5 2.3 pad_maximum_fusion.wr_ref
  5.8 0.0 copy-done.3
  5.8 0.0 copy-done.2
  5.8 0.0 copy-done.1
  5.8 0.0 copy-start.5
  5.9 0.0 copy-start.6
  5.9 0.8 pad_maximum_fusion.1.wq_ref
  6.7 0.0 copy-done.15
  6.7 0.0 copy-done.14
  6.7 0.0 copy-done.13
  6.7 0.6 broadcast_in_dim.2.bias_ref
  7.3 102.6 %gather.1 = (bf16[2,1024,512]{2,1,0:T(8,128)(2,1)}, bf16[4,512,384]{2,1,0:T(8,128)(2,1)}, bf16[4,1152,512]{2,1,0:T(8,128)(2,1)}, f32[4,8,768]{2,1,0:T(8,128)}) custom-call(bf16[768,512]{1,0:T(8,128)(2,1)} %x_ref.5, bf16[512,384]{1,0:T(8,128)(2,1)} %pad_maximum_fusion.1.wq_ref, bf16[1152,512]{1,0:T(8,128)(2,1)} %pad_maximum_fusion.wr_ref, ...), custom_call_target="tpu_custom_call" | custom-call | tf_op jit(solution)/shard_map/gather/pallas_call | solution.py:170
  109.9 0.0 copy-done.8
  109.9 0.0 copy-done.5
  109.9 0.0 copy-done.6
  109.9 0.6 stack.41.g1_ref.vec_ref
  110.5 0.0 copy-start.11
  110.6 0.0 copy-start.12
  110.6 0.0 copy-start.9
  110.6 0.0 copy-start.10
  110.6 26.2 %attend.1 = (bf16[3,1024,512]{2,1,0:T(8,128)(2,1)}, bf16[3,1024,384]{2,1,0:T(8,128)(2,1)}, bf16[3,2,1024,1024]{3,2,1,0:T(8,128)(2,1)}, f32[3,8,1024]{2,1,0:T(8,1...) custom-call(s32[3]{0:T(128)} %fusion.5.slot_ref, s32[4]{0:T(128)} %copy-done.8, ...), custom_call_target="tpu_custom_call" | custom-call | tf_op jit(solution)/shard_map/attend/pallas_call | solution.py:228
  136.7 19.4 %heads_out.1.mix_ref = bf16[768,512]{1,0:T(8,128)(2,1)} custom-call(bf16[3,1024,128]{2,1,0:T(8,128)(2,1)} %get-tuple-element.57.o_ref), custom_call_target="tpu_custom_call" | custom-call | tf_op jit(solution)/shard_map/heads_out/pallas_call | solution.py:299
  156.8 1.0 fusion.3.mask_ref
  157.8 0.0 copy-done.11
  157.8 0.0 copy-done.12
  157.8 0.0 copy-done.9
  157.8 0.0 copy-done.10
  157.8 0.6 stack.49.vec_ref
  158.5 21.0 %middle.1 = (bf16[768,512]{1,0:T(8,128)(2,1)}, f32[768,512]{1,0:T(8,128)}, bf16[768,512]{1,0:T(8,128)(2,1)}, bf16[4,1152,512]{2,1,0:T(8,128)(2,1)}, f32[16,512]{1,0:T(8,128)}) custom-call(bf16[768,512]{1,0:T(8,128)(2,1)} %x_ref.5, bf16[768,512]{1,0:T(8,128)(2,1)} %cot_ref.1, f32[768,1]{1,0:T(8,128)} %fusion.3.mask_ref, bf16[768,512]{1,0:T(8,128)(2,1)} %heads_out.1.mix_ref, ...), custom_call_target="tpu_custom_call" | custom-call | tf_op jit(solution)/shard_map/middle/pallas_call | solution.py:464
  179.5 19.1 %heads_in.1.do_ref = bf16[3,1024,128]{2,1,0:T(8,128)(2,1)} custom-call(bf16[768,512]{1,0:T(8,128)(2,1)} %get-tuple-element.61.do_ref), custom_call_target="tpu_custom_call" | custom-call | tf_op jit(solution)/shard_map/heads_in/pallas_call | solution.py:347
  198.6 22.4 %attend_back.1 = (bf16[4,512,384]{2,1,0:T(8,128)(2,1)}, f32[2,1024,512]{2,1,0:T(8,128)}, f32[4,8,384]{2,1,0:T(8,128)}) custom-call(s32[3]{0:T(128)} %fusion.5.slot_ref, s32[4]{0:T(128)} %copy-done.8, bf16[3,1024,128]{2,1,0:T(8,128)(2,1)} %heads_in.1.do_ref, bf16[3,1024,384]{2,1,0:T(8,128)(2,1)} %get-tuple-element.62.qkv_ref, ...), custom_call_target="tpu_custom_call" | custom-call | tf_op jit(solution)/shard_map/attend_back/pallas_call | solution.py:551
  221.0 3.8 %convert_element_type.32.pn_ref = bf16[2,1024,512]{2,1,0:T(8,128)(2,1)} convert(f32[2,1024,512]{2,1,0:T(8,128)} %get-tuple-element.67) | non-fusion elementwise | flops 1048576 | bytes 6291456 | tf_op jit(solution)/shard_map/convert_element_type | solution.py:760
  224.9 25.0 %rows_back.1 = (bf16[768,512]{1,0:T(8,128)(2,1)}, bf16[768,512]{1,0:T(8,128)(2,1)}) custom-call(bf16[2,1024,512]{2,1,0:T(8,128)(2,1)} %convert_element_type.32.pn_ref), custom_call_target="tpu_custom_call" | custom-call | tf_op jit(solution)/shard_map/rows_back/pallas_call | solution.py:389
  249.9 0.0 copy-start.4
  249.9 0.0 copy-start.7
  249.9 4.3 %first_back.1 = (bf16[768,512]{1,0:T(8,128)(2,1)}, f32[8,512]{1,0:T(8,128)}) custom-call(bf16[768,512]{1,0:T(8,128)(2,1)} %x_ref.5, f32[768,512]{1,0:T(8,128)} %get-tuple-element.60.gres_ref, bf16[768,512]{1,0:T(8,128)(2,1)} %get-tuple-element.68.own_ref, bf16[768,512]{1,0:T(8,128)(2,1)} %get-tuple-element.69.got_ref, f32[8,512]{1,0:T(8,128)} %stack.41.g1_ref.vec_ref), custom_call_target="tpu_custom_call" | custom-call | tf_op jit(solution)/shard_map/first_back/pallas_call | solution.py:605
  254.2 0.7 slice.66
  254.9 0.0 copy-done.4
  254.9 0.0 copy-done.7
  254.9 0.6 select_maximum_fusion.s_ref
  255.6 74.1 %reduce.3 = (bf16[512,384]{1,0:T(8,128)(2,1)}, bf16[1152,512]{1,0:T(8,128)(2,1)}, f32[16,512]{1,0:T(8,128)}) custom-call(bf16[4,512,384]{2,1,0:T(8,128)(2,1)} %get-tuple-element.71.q_ref, bf16[4,1152,512]{2,1,0:T(8,128)(2,1)} %get-tuple-element.72.r_ref, f32[16,512]{1,0:T(8,128)} %select_maximum_fusion.s_ref), custom_call_target="tpu_custom_call" | custom-call | tf_op jit(solution)/shard_map/reduce/pallas_call | solution.py:719
  329.6 0.0 copy-start
  329.6 2.9 fusion.8
  332.5 0.0 copy-done
  332.5 0.9 fusion.9
  333.4 1.6 slice.89
  335.0 1.5 fusion.10
  336.6 1.3 dynamic-slice_bitcast_fusion
  (7 shorter events, 0.0 us)
Async XLA Ops:
  0.7 5.2 %copy-start.3 = (bf16[512,128]{1,0:T(8,128)(2,1)S(1)}, bf16[512,128]{1,0:T(8,128)(2,1)}, u32[]{:S(2)}) copy-start(bf16[512,128]{1,0:T(8,128)(2,1)} %param.27) | copy-start | bytes 393220
  0.7 5.2 %copy-start.2 = (bf16[512,128]{1,0:T(8,128)(2,1)S(1)}, bf16[512,128]{1,0:T(8,128)(2,1)}, u32[]{:S(2)}) copy-start(bf16[512,128]{1,0:T(8,128)(2,1)} %param.29) | copy-start | bytes 393220
  0.7 5.2 %copy-start.1 = (bf16[512,128]{1,0:T(8,128)(2,1)S(1)}, bf16[512,128]{1,0:T(8,128)(2,1)}, u32[]{:S(2)}) copy-start(bf16[512,128]{1,0:T(8,128)(2,1)} %param.30) | copy-start | bytes 393220
  0.7 6.0 %copy-start.15 = (bf16[128]{0:T(256)(128)(2,1)S(1)}, bf16[128]{0:T(256)(128)(2,1)}, u32[]{:S(2)}) copy-start(bf16[128]{0:T(256)(128)(2,1)} %param.28) | copy-start | bytes 772
  0.7 6.0 %copy-start.14 = (bf16[128]{0:T(256)(128)(2,1)S(1)}, bf16[128]{0:T(256)(128)(2,1)}, u32[]{:S(2)}) copy-start(bf16[128]{0:T(256)(128)(2,1)} %param.31) | copy-start | bytes 772
  0.7 6.0 %copy-start.13 = (bf16[512]{0:T(512)(128)(2,1)S(1)}, bf16[512]{0:T(512)(128)(2,1)}, u32[]{:S(2)}) copy-start(bf16[512]{0:T(512)(128)(2,1)} %param.37) | copy-start | bytes 3076
  2.3 107.6 %copy-start.8 = (s32[4]{0:T(128)}, s32[4]{0:T(128)S(1)}, u32[]{:S(2)}) copy-start(s32[4]{0:T(128)S(1)} %constant_dynamic-update-slice_fusion.shard_ref) | copy-start | bytes 52
  5.8 104.1 %copy-start.5 = (f32[512]{0:T(512)S(1)}, f32[512]{0:T(512)}, u32[]{:S(2)}) copy-start(f32[512]{0:T(512)} %param.25) | copy-start | bytes 6148
  5.9 104.1 %copy-start.6 = (f32[512]{0:T(512)S(1)}, f32[512]{0:T(512)}, u32[]{:S(2)}) copy-start(f32[512]{0:T(512)} %param.26) | copy-start | bytes 6148
  110.5 47.3 %copy-start.11 = (bf16[512]{0:T(512)(128)(2,1)S(1)}, bf16[512]{0:T(512)(128)(2,1)}, u32[]{:S(2)}) copy-start(bf16[512]{0:T(512)(128)(2,1)} %param.33) | copy-start | bytes 3076
  110.6 47.3 %copy-start.12 = (bf16[512]{0:T(512)(128)(2,1)S(1)}, bf16[512]{0:T(512)(128)(2,1)}, u32[]{:S(2)}) copy-start(bf16[512]{0:T(512)(128)(2,1)} %param.39) | copy-start | bytes 3076
  110.6 47.3 %copy-start.9 = (f32[512]{0:T(512)S(1)}, f32[512]{0:T(512)}, u32[]{:S(2)}) copy-start(f32[512]{0:T(512)} %param.34) | copy-start | bytes 6148
  110.6 47.3 %copy-start.10 = (f32[512]{0:T(512)S(1)}, f32[512]{0:T(512)}, u32[]{:S(2)}) copy-start(f32[512]{0:T(512)} %param.35) | copy-start | bytes 6148
  249.9 5.0 %copy-start.4 = (f32[4,8,384]{2,1,0:T(8,128)S(1)}, f32[4,8,384]{2,1,0:T(8,128)}, u32[]{:S(2)}) copy-start(f32[4,8,384]{2,1,0:T(8,128)} %get-tuple-element.75) | copy-start | bytes 147460
  249.9 5.0 %copy-start.7 = (f32[16,512]{1,0:T(8,128)S(1)}, f32[16,512]{1,0:T(8,128)}, u32[]{:S(2)}) copy-start(f32[16,512]{1,0:T(8,128)} %get-tuple-element.74) | copy-start | bytes 98308
  329.6 2.9 copy-start

commit v2 on v0

v2 whole, which is shorter than its diff:
```python
import functools

import jax
import jax.numpy as jnp
from jax import lax
from jax.experimental import pallas as pl
from jax.experimental.pallas import tpu as pltpu
from jax.sharding import PartitionSpec as P

HEAD = 64
PATCH = 1024
PAIR = 2 * HEAD
EPSILON = 1e-06
MESH = pl.DeviceIdType.MESH
BF16 = jnp.bfloat16
F32 = jnp.float32
GELU_C = 0.7978845608028654
GELU_A = 0.044715

SEGMENTS = (
    ((0, 768, 0, 0, 1),),
    ((0, 256, 0, 768, 0), (256, 512, 1, 0, 2)),
    ((0, 512, 1, 512, 1), (512, 256, 0, 0, 3)),
    ((0, 768, 0, 256, 2),),
)
TASKS = (
    ((0, 0), (0, 1), (0, 2)),
    ((1, 1), (1, 0), (0, 3)),
    ((1, 2), (1, 3), (0, 0)),
    ((0, 3), (0, 2), (0, 1)),
)
ANY = pl.BlockSpec(memory_space=pl.ANY)


def partner_segment(me, slot):
    other = [seg[4] for seg in SEGMENTS[me] if seg[2] == slot][0]
    return other, [seg for seg in SEGMENTS[other] if seg[4] == me and seg[2] == slot][0]


def nt_dot(a, b):
    return lax.dot_general(a, b, (((1,), (1,)), ((), ())), preferred_element_type=F32)


def tn_dot(a, b):
    return lax.dot_general(a, b, (((0,), (0,)), ((), ())), preferred_element_type=F32)


def nn_dot(a, b):
    return jnp.dot(a, b, preferred_element_type=F32)


def place():
    d, m = lax.axis_index("dp"), lax.axis_index("mp")
    core, b1, b2 = d % 2, (d // 2) % 2, (d // 4) % 2
    lo = b1 + core * (b2 - b1)
    hi = b2 + core * (b1 - b2)
    flip_lo = d + (1 - core) * (2 - 4 * b1) + core * (4 - 8 * b2)
    flip_hi = d + (1 - core) * (4 - 8 * b2) + core * (2 - 4 * b1)
    flip_core = d + 1 - 2 * core
    return d, m, core, lo, hi, flip_lo, flip_hi, flip_core


def barrier(targets):
    sem = pltpu.get_barrier_semaphore()
    for dev in targets:
        pl.semaphore_signal(sem, inc=1, device_id=dev, device_id_type=MESH)
    pl.semaphore_wait(sem, len(targets))


VMEM_LIMIT = 63 << 20


class Copies:
    def __init__(self, send, recv):
        self.send, self.recv, self.all, self.done = send, recv, [], []

    def make(self, src, dst, dev):
        i = len(self.all)
        c = pltpu.make_async_remote_copy(src, dst, self.send.at[i], self.recv.at[i],
                                         device_id=dev, device_id_type=MESH)
        self.all.append(c)
        return c

    def push(self, src, dst, dev):
        c = self.make(src, dst, dev)
        c.start()
        return c

    def exchange(self, src, dst, dev):
        c = self.make(src, dst, dev)
        c.start()
        c.wait()
        self.done.append(c)

    def finish(self):
        for c in self.all:
            if not any(c is o for o in self.done):
                c.wait_send()


def start(copies):
    for c in copies:
        c.start()


def arrive(copies):
    for c in copies:
        c.wait_recv()


FORWARD_CHUNKS = 2


def layer_kernel(n_high, live_ref, x_ref, cot_ref, wq_ref, wk_ref, wv_ref, wo_ref, up_ref, down_ref, vec_ref,
                 out_ref, gt_ref, oq_ref, or_ref, os_ref, p_ref,
                 tok, ent_ref, gq_ref, gr_ref, gb_ref, qkv_ref, l_ref, ot_ref, mix_ref, kt_sc, qt_sc, vt_sc,
                 p_sc, o_sc, e2_sc, res_sc, xhat_sc, rstd_sc, do_sc, dr_ref,
                 dot_in, dkv_sc, pn_sc, pnb_sc, got_sc,
                 dq_sc, q3, q2, q1, qz, r3, r2, r1, rz, rh, qh, s_all, s_z, s_h,
                 psem, lsem, send, recv, tsend, trecv, osend, orecv, dsend, drecv, bsend, brecv):
    d, m, core, lo, hi, flip_lo, flip_hi, flip_core = place()
    others = [(m + j) % 4 for j in (1, 2, 3)]
    froms = [(m + 3) % 4, (m + 2) % 4, (m + 1) % 4]
    cp = Copies(send, recv)
    base, at = (d // 8) * 8, d % 8
    plane = [base + (at + j) % 8 for j in range(1, 8)]
    highs = []
    for b in range(n_high):
        step = 8 * 2 ** b
        bit = (d // step) % 2
        highs.append(d + step - 2 * step * bit)
    rq, rr = gq_ref.shape[1] // 8, gr_ref.shape[1] // 8
    piece = 4 * core + 2 * hi + lo
    second, third = m + 1 - 2 * (m % 2), (m + 2) % 4
    middle_rank = (m % 3 > 0).astype(jnp.int32)
    n_out, n_up = wo_ref.shape[0], up_ref.shape[0]

    def rows(first, n, size):
        return pl.ds(pl.multiple_of(first * size, 16), n * size)

    gr_ref[m, 0:n_out, :] = wo_ref[...]
    gr_ref[m, n_out:n_out + n_up, :] = up_ref[...]
    gr_ref[m, n_out + n_up:, :] = down_ref[...]
    gq_ref[m, :, 0:PAIR] = wq_ref[...]
    gq_ref[m, :, PAIR:2 * PAIR] = wk_ref[...]
    gq_ref[m, :, 2 * PAIR:] = wv_ref[...]
    gb_ref[m] = vec_ref[8:16, :]

    steps = ((flip_lo, piece, 1), (flip_hi, 4 * core + 2 * hi, 2), (flip_core, 4 * core, 4))
    part = gq_ref.at[m, rows(piece, 1, rq), :]
    waves_q = [[cp.make(part, part, (d, dev)) for dev in (second, third)]]
    waves_b = [cp.make(vec_ref.at[pl.ds(8, 8), :], gb_ref.at[m], (d, o)) for o in others]
    for dev, first, n in steps:
        parts = [gq_ref.at[sh, rows(first, n, rq), :] for sh in (second, third)]
        waves_q.append([cp.make(part, part, (dev, m)) for part in parts])
    waves_r = []
    wide = gr_ref.shape[2] // FORWARD_CHUNKS
    for c in range(FORWARD_CHUNKS):
        cols = pl.ds(c * wide, wide)
        part = gr_ref.at[m, rows(piece, 1, rr), cols]
        ws = [[cp.make(part, part, (d, o)) for o in others]]
        for dev, first, n in steps:
            parts = [gr_ref.at[sh, rows(first, n, rr), cols] for sh in froms]
            ws.append([cp.make(part, part, (dev, m)) for part in parts])
        waves_r.append(ws)

    def pass_on(waves, st):
        for before, after in zip(waves[st - 1], waves[st]):
            before.wait_recv()
            after.start()

    def token_copy(k, i):
        ls, n, slot, fs, other = SEGMENTS[k][i]
        return pltpu.make_async_remote_copy(
            x_ref.at[pl.ds(ls, n), :], tok.at[slot, pl.ds(fs, n), :],
            tsend.at[i], trecv.at[slot], device_id=(d, other), device_id_type=MESH)

    barrier([(d, o) for o in others] + [(o, m) for o in plane] + [(h, m) for h in highs])
    start(waves_q[0])
    for k in range(4):
        @pl.when(m == k)
        def _():
            for i in sorted(range(len(SEGMENTS[k])), key=lambda i: -SEGMENTS[k][i][2]):
                token_copy(k, i).start()
    start(waves_b)
    gain, shift = vec_ref[0:1, :], vec_ref[1:2, :]

    def norm_rows(n, ref, ls, slot, fs):
        def block(i, carry):
            r = pl.multiple_of(i * 256, 256)
            x = ref[pl.ds(ls + r, 256), :].astype(F32)
            cen = x - jnp.mean(x, axis=-1, keepdims=True)
            var = jnp.mean(cen * cen, axis=-1, keepdims=True)
            xhat = cen * lax.rsqrt(var + EPSILON)
            tok[slot, pl.ds(fs + r, 256), :] = xhat.astype(BF16)
            ent_ref[slot, pl.ds(fs + r, 256), :] = (xhat * gain + shift).astype(BF16)
            return carry

        lax.fori_loop(0, n // 256, block, 0)

    for k in range(4):
        @pl.when(m == k)
        def _():
            for ls, n, slot, fs, other in SEGMENTS[k]:
                norm_rows(n, x_ref, ls, slot, fs)

    def remote_rows(slot_wanted):
        for k in range(4):
            @pl.when(m == k)
            def _():
                for i, (ls, n, slot, fs, other) in enumerate(SEGMENTS[k]):
                    if slot == slot_wanted[k]:
                        _, (pls, pn, _, pfs, _) = partner_segment(k, slot)
                        part = tok.at[slot, pl.ds(pfs, pn), :]
                        pltpu.make_async_remote_copy(part, part, tsend.at[i], trecv.at[slot],
                                                     device_id=(d, other), device_id_type=MESH).wait_recv()
                        norm_rows(pn, tok.at[slot], pfs, slot, pfs)

    lane = lax.broadcasted_iota(jnp.int32, (1, PAIR), 1)

    def spill(t, h):
        return pltpu.make_async_copy(p_sc.at[h], p_ref.at[t, h], psem.at[h])

    def out_copy(k, t):
        slot, pair = TASKS[k][t]
        other, (pls, pn, _, pfs, _) = partner_segment(k, slot)
        return pltpu.make_async_remote_copy(
            o_sc.at[t, pl.ds(pfs, pn), :], mix_ref.at[pair, pl.ds(pls, pn), :],
            osend.at[t], orecv.at[slot, pair], device_id=(d, other), device_id_type=MESH)

    def keep_copy(k, t):
        slot, pair = TASKS[k][t]
        ls, n, _, fs, _ = [seg for seg in SEGMENTS[k] if seg[2] == slot][0]
        return pltpu.make_async_copy(o_sc.at[t, pl.ds(fs, n), :], mix_ref.at[pair, pl.ds(ls, n), :], lsem.at[t])

    pass_on(waves_q, 1)
    remote_rows((0, 1, 1, 0))
    for ws in waves_r:
        start(ws[0])

    schedule = {
        (0, 1): lambda: pass_on(waves_q, 2),
        (0, 2): lambda: pass_on(waves_q, 3),
        (0, 4): lambda: pass_on(waves_r[0], 1),
        (1, 1): lambda: pass_on(waves_r[1], 1),
        (1, 3): lambda: pass_on(waves_r[0], 2),
        (2, 1): lambda: pass_on(waves_r[1], 2),
        (2, 3): lambda: pass_on(waves_r[0], 3),
    }

    def task(t, carry):
        slot = middle_rank * (1 - t // 2)
        shard = m + (t % 2) * (second - m) + (t // 2) * (third - m)

        def point(i):
            for tt in range(3):
                if (tt, i) in schedule:
                    @pl.when(t == tt)
                    def _():
                        schedule[tt, i]()

        @pl.when(t == 1)
        def _():
            arrive(waves_b)
            waves_q[3][0].wait_recv()

        @pl.when(t == 2)
        def _():
            waves_q[3][1].wait_recv()
            remote_rows((1, 0, 0, 1))

        ent = ent_ref[slot]
        bias = gb_ref[shard, 0:1, :]
        q = (nn_dot(ent, gq_ref[shard, :, 0:PAIR]) + bias[:, 0:PAIR]).astype(BF16)
        k = nn_dot(ent, gq_ref[shard, :, PAIR:2 * PAIR]).astype(BF16)
        v = (nn_dot(ent, gq_ref[shard, :, 2 * PAIR:]) + bias[:, PAIR:2 * PAIR]).astype(BF16)
        qs = q * jnp.asarray(HEAD ** -0.5, BF16)
        qkv_ref[t, :, 0:PAIR] = qs
        qkv_ref[t, :, PAIR:2 * PAIR] = k
        qkv_ref[t, :, 2 * PAIR:] = v
        for h in range(2):
            kt_sc[h] = jnp.where((lane // HEAD) == h, k, jnp.zeros_like(k))
        qt_sc[...] = qs.astype(F32).T.astype(BF16)
        vt_sc[...] = v.astype(F32).T.astype(BF16)
        point(0)

        for h in range(2):
            @pl.when(t > 0)
            def _():
                spill(t - 1, h).wait()

            st = nn_dot(kt_sc[h], qt_sc[...])
            peak = jnp.max(st, axis=0, keepdims=True)
            raised = jnp.exp(st - peak)
            l_ref[t, h:h + 1, :] = 1.0 / jnp.sum(raised, axis=0, keepdims=True)
            p_sc[h] = raised.astype(BF16)
            spill(t, h).start()
            point(1 + h)
        for h in range(2):
            part = slice(h * HEAD, (h + 1) * HEAD)
            ot_ref[t, part, :] = nn_dot(vt_sc[part, :], p_sc[h]) * l_ref[t, h:h + 1, :]
            point(3 + h)
        o_sc[t] = ot_ref[t].T.astype(BF16)
        for k in range(4):
            @pl.when(m == k)
            def _():
                for tt in range(3):
                    @pl.when(t == tt)
                    def _():
                        out_copy(k, tt).start()
                        keep_copy(k, tt).start()
        return carry

    lax.fori_loop(0, 3, task, 0)
    for ws in waves_r[1:]:
        pass_on(ws, 3)
    for h in range(2):
        spill(2, h).wait()
    n_rows = x_ref.shape[0]
    row = m * n_rows + lax.broadcasted_iota(jnp.int32, (n_rows, 1), 0)
    mask = (row // PATCH < live_ref[0]).astype(F32)
    gf_sc = p_sc.at[1, pl.ds(0, n_rows), pl.ds(512, 512)]
    e2_in = p_sc.at[1, pl.ds(0, n_rows), pl.ds(0, 512)]
    e2t_sc = p_sc.at[0, pl.ds(0, 512), pl.ds(0, n_rows)]
    gf_sc[...] = (mask * cot_ref[...].astype(F32)).astype(BF16)
    os_ref[...] = jnp.zeros_like(os_ref)
    os_ref[5:6, :] = jnp.sum(gf_sc[...].astype(F32), axis=0, keepdims=True)
    for k in range(4):
        @pl.when(m == k)
        def _():
            for ls, n, slot, fs, other in SEGMENTS[k]:
                for slot2, pair in TASKS[other]:
                    if slot2 == slot:
                        part = mix_ref.at[pair, pl.ds(ls, n), :]
                        pltpu.make_async_remote_copy(
                            part, part, osend.at[0], orecv.at[slot, pair],
                            device_id=(d, other), device_id_type=MESH).wait_recv()
            for t in range(3):
                keep_copy(k, t).wait()
    for ws in waves_r:
        arrive(ws[3])


    wo = jnp.concatenate([gr_ref[s, 0:PAIR, :] for s in range(4)], axis=0)
    mix = jnp.concatenate([mix_ref[i] for i in range(4)], axis=1)
    res = x_ref[...].astype(F32) + nn_dot(mix, wo) + vec_ref[4:5, :]
    cen = res - jnp.mean(res, axis=-1, keepdims=True)
    var = jnp.mean(cen * cen, axis=-1, keepdims=True)
    rstd = lax.rsqrt(var + EPSILON)
    xhat = cen * rstd
    e2 = (xhat * vec_ref[2:3, :] + vec_ref[3:4, :]).astype(BF16)
    e2_in[...] = e2
    e2t_sc[...] = e2.astype(F32).T.astype(BF16)
    res_sc[...] = res
    xhat_sc[...] = xhat
    rstd_sc[...] = jnp.broadcast_to(rstd, rstd_sc.shape)

    def hidden(s, carry):
        up = gr_ref[s, PAIR:PAIR + 512, :]
        down = gr_ref[s, PAIR + 512:, :]
        pre = nn_dot(e2_in[...], up) + gb_ref[s, 1:2, :]
        sq = pre * pre
        th = jnp.tanh(GELU_C * pre * (1.0 + GELU_A * sq))
        half = 0.5 * (1.0 + th)
        act = (pre * half).astype(BF16)
        slope = half + (0.5 * GELU_C) * pre * (1.0 - th * th) * (1.0 + (3.0 * GELU_A) * sq)
        gp = (slope * nt_dot(gf_sc[...], down)).astype(BF16)
        feed = nn_dot(act, down)
        gn = nt_dot(gp, up)

        @pl.when(s == 0)
        def _():
            pn_sc[0, 0:n_rows, :] = feed
            pn_sc[1, 0:n_rows, :] = gn

        @pl.when(s > 0)
        def _():
            pn_sc[0, 0:n_rows, :] += feed
            pn_sc[1, 0:n_rows, :] += gn

        dr_ref[s, PAIR:PAIR + 512, :] = nn_dot(e2t_sc[...], gp).astype(BF16)
        dr_ref[s, PAIR + 512:, :] = tn_dot(act, gf_sc[...]).astype(BF16)
        os_ref[pl.ds(8 + s, 1), :] = jnp.sum(gp.astype(F32), axis=0, keepdims=True)
        return carry

    lax.fori_loop(0, 4, hidden, 0)
    gn = pn_sc[1, 0:n_rows, :]
    xhat = xhat_sc[...]
    gg = gn * vec_ref[2:3, :]
    mg = jnp.mean(gg, axis=-1, keepdims=True)
    mx = jnp.mean(gg * xhat, axis=-1, keepdims=True)
    gres = mask * cot_ref[...].astype(F32) + rstd_sc[:, 0:1] * (gg - mg - xhat * mx)
    ga = gres.astype(BF16)
    do = nt_dot(ga, wo).astype(BF16)
    for s in range(4):
        do_sc[s] = do[:, s * PAIR:(s + 1) * PAIR]

    slots = (middle_rank, middle_rank, 0)
    shards = (m, second, third)
    order = (2, 0, 1)
    last_task = order[2]

    def head_copies(k):
        out, n_sent = [], 0
        for t in order:
            for ls, n, slot, fs, other in SEGMENTS[k]:
                slot2, pair = TASKS[other][t]
                if slot2 == slot:
                    out.append(pltpu.make_async_remote_copy(
                        do_sc.at[pair, pl.ds(ls, n), :], dot_in.at[t, pl.ds(fs, n), :],
                        dsend.at[n_sent], drecv.at[t], device_id=(d, other), device_id_type=MESH))
                    n_sent += 1
        return out

    def own_head(k, t):
        slot, pair = TASKS[k][t]
        ls, n, _, fs, _ = [seg for seg in SEGMENTS[k] if seg[2] == slot][0]
        return pltpu.make_async_copy(do_sc.at[pair, pl.ds(ls, n), :], dot_in.at[t, pl.ds(fs, n), :], lsem.at[t])

    for k in range(4):
        @pl.when(m == k)
        def _():
            for c in head_copies(k):
                c.start()
            for t in range(3):
                own_head(k, t).start()

    def fetch(t, h):
        return pltpu.make_async_copy(p_ref.at[t, h], p_sc.at[h], psem.at[h])

    for h in range(2):
        fetch(order[0], h).start()

    halves = (
        (flip_core, 4 * (1 - core), 4 * core, 4),
        (flip_hi, 4 * core + 2 * (1 - hi), 4 * core + 2 * hi, 2),
        (flip_lo, 4 * core + 2 * hi + 1 - lo, piece, 1),
    )

    class Flow:
        def __init__(self, c):
            self.c, self.lanes = c, slice(256 * c, 256 * c + 256)
            cols = pl.ds(256 * c, 256)
            self.half = [cp.make(dr_ref.at[:, rows(away, n, rr), cols], buf.at[c], (dev, m))
                         for (dev, away, mine, n), buf in zip(halves, (r3, r2, r1))]
            self.across = [cp.make(dr_ref.at[others[j], rows(piece, 1, rr), cols], rz.at[c, j], (d, others[j]))
                           for j in range(3)]
            parts = [or_ref.at[rows(first, n, rr), cols] for dev, first, n in steps]
            self.double = [cp.make(part, part, (dev, m)) for part, (dev, first, n) in zip(parts, steps)]

        def run(self, st):
            c, lanes = self.c, self.lanes
            if st == 0:
                self.half[0].start()
            elif st <= 3:
                dev, away, mine, n = halves[st - 1]
                buf = (r3, r2, r1)[st - 1]
                self.half[st - 1].wait_recv()

                def add(s, carry):
                    sl = rows(mine, n, rr)
                    dr_ref[s, sl, lanes] = (dr_ref[s, sl, lanes].astype(F32) + buf[c, s].astype(F32)).astype(BF16)
                    return carry

                lax.fori_loop(0, 4, add, 0)
                if st < 3:
                    self.half[st].start()
                else:
                    start(self.across)
            elif st == 4:
                acc = dr_ref[m, rows(piece, 1, rr), lanes].astype(F32)
                for j in range(3):
                    self.across[j].wait_recv()
                    acc += rz[c, j].astype(F32)
                for b in range(n_high):
                    dr_ref[m, rows(piece, 1, rr), lanes] = acc.astype(BF16)
                    cp.exchange(dr_ref.at[m, rows(piece, 1, rr), pl.ds(256 * c, 256)], rh.at[c, b], (highs[b], m))
                    acc += rh[c, b].astype(F32)
                or_ref[rows(piece, 1, rr), lanes] = acc.astype(BF16)
                self.double[0].start()
            elif st <= 6:
                self.double[st - 5].wait_recv()
                self.double[st - 4].start()
            else:
                self.double[2].wait_recv()

    class HeadFlow:
        def __init__(self, t):
            self.t = t
            self.half = [cp.make(dq_sc.at[t, rows(away, n, rq), :], buf.at[t], (dev, m))
                         for (dev, away, mine, n), buf in zip(halves, (q3, q2, q1))]
            self.across = []
            if t > 0:
                self.across = [cp.make(dq_sc.at[t, rows(piece, 1, rq), :], qz.at[t - 1], (d, shards[t]))]

        def run(self, st):
            t = self.t
            if st > 0:
                dev, away, mine, n = halves[st - 1]
                self.half[st - 1].wait_recv()
                sl = rows(mine, n, rq)
                buf = (q3, q2, q1)[st - 1]
                dq_sc[t, sl, :] = (dq_sc[t, sl, :].astype(F32) + buf[t].astype(F32)).astype(BF16)
            if st < 3:
                self.half[st].start()
            else:
                start(self.across)

    flows = [Flow(0), Flow(1)]
    heads = [HeadFlow(t) for t in range(3)]
    gw = tn_dot(mix, ga).astype(BF16)
    for s in range(4):
        dr_ref[s, 0:PAIR, :] = gw[s * PAIR:(s + 1) * PAIR, :]
    flows[0].run(0)
    flows[1].run(0)
    os_ref[2:3, :] = jnp.sum(gn * xhat, axis=0, keepdims=True)
    os_ref[3:4, :] = jnp.sum(gn, axis=0, keepdims=True)
    os_ref[4:5, :] = jnp.sum(ga.astype(F32), axis=0, keepdims=True)
    out_ref[...] = (mask * (res_sc[...] + pn_sc[0, 0:n_rows, :] + vec_ref[5:6, :])).astype(BF16)
    res_sc[...] = gres
    for k in range(4):
        @pl.when(m == k)
        def _():
            for ls, n, slot, fs, other in SEGMENTS[k]:
                e2_sc[ls:ls + n, :] = tok[slot, fs:fs + n, :]

    def first_stats(i, carry):
        rs = pl.ds(pl.multiple_of(i * 256, 256), 256)
        x = x_ref[rs, :].astype(F32)
        cen = x - jnp.mean(x, axis=-1, keepdims=True)
        rstd = lax.rsqrt(jnp.mean(cen * cen, axis=-1, keepdims=True) + EPSILON)
        rstd_sc[rs, :] = jnp.broadcast_to(rstd, (256, 128))
        return carry

    lax.fori_loop(0, n_rows // 256, first_stats, 0)
    flows[0].run(1)

    def row_copy(k, i):
        ls, n, slot, fs, other = SEGMENTS[k][i]
        _, (pls, pn, _, pfs, _) = partner_segment(k, slot)
        return pltpu.make_async_remote_copy(
            pnb_sc.at[pl.ds(slot * n_rows, pn), :], got_sc.at[pl.ds(pls, pn), :],
            bsend.at[i], brecv.at[slot], device_id=(d, other), device_id_type=MESH)

    def norm_sums(slot):
        def block(i, carry):
            rs = pl.ds(pl.multiple_of(i * 256, 256), 256)
            gn = pn_sc[slot, rs, :]
            gain_sum, bias_sum = carry
            return (gain_sum + jnp.sum(gn * tok[slot, rs, :].astype(F32), axis=0, keepdims=True),
                    bias_sum + jnp.sum(gn, axis=0, keepdims=True))

        zero = jnp.zeros((1, 512), F32)
        gain_sum, bias_sum = lax.fori_loop(0, PATCH // 256, block, (zero, zero))
        os_ref[0:1, :] += gain_sum
        os_ref[1:2, :] += bias_sum

    back_schedule = {
        (0, 1): lambda: flows[1].run(1),
        (0, 2): lambda: flows[0].run(2),
        (1, 0): lambda: flows[1].run(2),
        (1, 1): lambda: (flows[0].run(3), heads[2].run(1)),
        (1, 2): lambda: (flows[1].run(3), heads[2].run(2)),
        (2, 0): lambda: flows[0].run(4),
        (2, 1): lambda: (heads[2].run(3), heads[0].run(1)),
        (2, 2): lambda: (flows[1].run(4), heads[0].run(2), flows[0].run(5)),
    }
    width = 256

    def back_task(step, carry):
        t = (step + 2) % 3
        slot = middle_rank * (1 - t // 2)
        shard = m + (t % 2) * (second - m) + (t // 2) * (third - m)

        def at_step(i, what):
            @pl.when(step == i)
            def _():
                what()

        def point(i):
            for st in range(3):
                if (st, i) in back_schedule:
                    at_step(st, back_schedule[st, i])

        for k in range(4):
            @pl.when(m == k)
            def _():
                for st in range(3):
                    @pl.when(step == st)
                    def _():
                        tt = order[st]
                        slot_k, pair = TASKS[k][tt]
                        other, (pls, pn, _, pfs, _) = partner_segment(k, slot_k)
                        part = dot_in.at[tt, pl.ds(pfs, pn), :]
                        pltpu.make_async_remote_copy(part, part, dsend.at[0], drecv.at[tt],
                                                     device_id=(d, other), device_id_type=MESH).wait_recv()
                        own_head(k, tt).wait()
        dot_full = dot_in[t].astype(F32).T
        scaled = jnp.concatenate(
            [dot_full[0:HEAD] * l_ref[t, 0:1, :], dot_full[HEAD:] * l_ref[t, 1:2, :]], axis=0)
        qt_sc[...] = scaled.astype(BF16)
        point(0)
        qs = qkv_ref[t, :, 0:PAIR]
        k = qkv_ref[t, :, PAIR:2 * PAIR]
        v = qkv_ref[t, :, 2 * PAIR:]
        zero = jnp.zeros_like(k)
        dqt = []
        for h in range(2):
            fetch(t, h).wait()
            sel = (lane // HEAD) == h
            part = slice(h * HEAD, (h + 1) * HEAD)
            vm = jnp.where(sel, v, zero)
            center = jnp.sum(qt_sc[part, :].astype(F32) * ot_ref[t, part, :], axis=0, keepdims=True)
            dop = qt_sc[...].astype(F32).T.astype(BF16)
            dv = nn_dot(p_sc[h], jnp.where(sel, dop, zero))
            for c in range(PATCH // width):
                cols = slice(c * width, (c + 1) * width)
                dpt = nn_dot(vm, qt_sc[:, cols])
                p_sc[h, :, cols] = (p_sc[h, :, cols].astype(F32) * (dpt - center[:, cols])).astype(BF16)
            kt = k.astype(F32).T.astype(BF16)
            dqt.append(nn_dot(kt[part], p_sc[h]))
            dk = nn_dot(p_sc[h], jnp.where(sel, qs, zero))

            @pl.when(step < 2)
            def _():
                fetch((step + 3) % 3, h).start()

            if h == 0:
                dkv_sc[0] = dk
                dkv_sc[1] = dv
            point(1 + h)
        dq = (jnp.concatenate(dqt, axis=0) * HEAD ** -0.5).T
        dqkv = jnp.concatenate(
            [dq.astype(BF16), (dkv_sc[0] + dk).astype(BF16), (dkv_sc[1] + dv).astype(BF16)], axis=1)
        back = nt_dot(dqkv, gq_ref[shard])
        first = (step == 0) | ((step == 1) & (middle_rank == 1))

        @pl.when(first)
        def _():
            pn_sc[slot] = back

        @pl.when(jnp.logical_not(first))
        def _():
            pn_sc[slot] += back

        for kk in range(4):
            last = {}
            for st in range(3):
                last[TASKS[kk][order[st]][0]] = st
            for i, (ls, n, slot_k, fs, other) in enumerate(SEGMENTS[kk]):
                @pl.when((m == kk) & (step == last[slot_k]))
                def _():
                    _, (pls, pn, _, pfs, _) = partner_segment(kk, slot_k)
                    pnb_sc[slot_k * n_rows:slot_k * n_rows + pn, :] = pn_sc[slot_k, pfs:pfs + pn, :].astype(BF16)
                    row_copy(kk, i).start()
                    xhat_sc[ls:ls + n, :] = pn_sc[slot_k, fs:fs + n, :]
        dq_sc[t] = tn_dot(ent_ref[slot], dqkv).astype(BF16)
        for st in range(3):
            at_step(st, functools.partial(heads[order[st]].run, 0))
        os_ref[pl.ds(12 + shard, 1), 0:384] = jnp.sum(dqkv.astype(F32), axis=0, keepdims=True)

        @pl.when((step == 2) | ((step == 0) & (middle_rank == 1)))
        def _():
            norm_sums(slot)

        return carry

    lax.fori_loop(0, 3, back_task, 0)
    s_all[7] = os_ref[...]
    wave = [cp.push(s_all.at[7], s_all.at[j], (plane[j], m)) for j in range(7)]
    flows[1].run(5)
    flows[0].run(6)
    heads[0].run(3)
    heads[1].run(1)
    acc = os_ref[...]
    for j in range(7):
        wave[j].wait_recv()
        acc += s_all[j]
    s_z[3] = acc
    wave = [cp.push(s_z.at[3], s_z.at[j], (d, others[j])) for j in range(3)]
    heads[1].run(2)
    flows[1].run(6)
    flows[0].run(7)
    heads[1].run(3)
    flows[1].run(7)
    for j in range(3):
        wave[j].wait_recv()
        acc += s_z[j]
    for b in range(n_high):
        s_h[0] = acc
        cp.exchange(s_h.at[0], s_h.at[1 + b], (highs[b], m))
        acc += s_h[1 + b]
    os_ref[...] = acc

    acc = dq_sc[0, rows(piece, 1, rq), :].astype(F32)
    for t in (1, 2):
        heads[t].across[0].wait_recv()
        acc += qz[t - 1].astype(F32)
    for b in range(n_high):
        dq_sc[0, rows(piece, 1, rq), :] = acc.astype(BF16)
        cp.exchange(dq_sc.at[0, rows(piece, 1, rq), :], qh.at[b], (highs[b], m))
        acc += qh[b].astype(F32)
    oq_ref[rows(piece, 1, rq), :] = acc.astype(BF16)

    def double_q(i):
        dev, first, n = steps[i]
        part = oq_ref.at[rows(first, n, rq), :]
        return cp.push(part, part, (dev, m))

    qw = double_q(0)

    for k in range(4):
        @pl.when(m == k)
        def _():
            for i, (ls, n, slot, fs, other) in enumerate(SEGMENTS[k]):
                part = got_sc.at[pl.ds(ls, n), :]
                pltpu.make_async_remote_copy(part, part, bsend.at[i], brecv.at[slot],
                                             device_id=(d, other), device_id_type=MESH).wait_recv()
    for r in range(0, n_rows, 256):
        rs = slice(r, r + 256)
        gn = xhat_sc[rs, :] + got_sc[rs, :].astype(F32)
        xhat = e2_sc[rs, :].astype(F32)
        gg = gn * vec_ref[0:1, :]
        mg = jnp.mean(gg, axis=-1, keepdims=True)
        mx = jnp.mean(gg * xhat, axis=-1, keepdims=True)
        gt_ref[rs, :] = (res_sc[rs, :] + rstd_sc[rs, 0:1] * (gg - mg - xhat * mx)).astype(BF16)
        if r < 512:
            qw.wait_recv()
            qw = double_q(1 + r // 256)
    qw.wait_recv()
    for k in range(4):
        @pl.when(m == k)
        def _():
            for t in range(3):
                out_copy(k, t).wait_send()
            for i in range(len(SEGMENTS[k])):
                token_copy(k, i).wait_send()
                row_copy(k, i).wait_send()
            for c in head_copies(k):
                c.wait_send()
    cp.finish()


def layer(n_high, live, x, cot, wq, wk, wv, wo, up, down, vec):
    dma = pltpu.SemaphoreType.DMA
    n = x.shape[0]
    cols_q, rows_r = 3 * PAIR, wo.shape[0] + up.shape[0] + down.shape[0]
    rq, rr = wq.shape[0] // 8, rows_r // 8
    high = max(n_high, 1)
    copies = 11 + FORWARD_CHUNKS * 12 + 2 * (9 + n_high) + 11 + 10 + 3 + 2 * n_high
    vmem = pl.BlockSpec(memory_space=pltpu.VMEM)
    ve = pltpu.VMEM
    return pl.pallas_call(
        functools.partial(layer_kernel, n_high),
        name="layer",
        out_shape=(
            jax.ShapeDtypeStruct((n, 512), BF16),
            jax.ShapeDtypeStruct((n, 512), BF16),
            jax.ShapeDtypeStruct((8 * rq, cols_q), BF16),
            jax.ShapeDtypeStruct((8 * rr, 512), BF16),
            jax.ShapeDtypeStruct((16, 512), F32),
            jax.ShapeDtypeStruct((3, 2, PATCH, PATCH), BF16),
        ),
        in_specs=[pl.BlockSpec(memory_space=pltpu.SMEM)] + [vmem] * 9,
        out_specs=(vmem,) * 5 + (ANY,),
        scratch_shapes=[
            ve((2, PATCH, 512), BF16), ve((2, PATCH, 512), BF16), ve((4, 8 * rq, cols_q), BF16),
            ve((4, 8 * rr, 512), BF16), ve((4, 8, 512), F32), ve((3, PATCH, cols_q), BF16), ve((3, 8, PATCH), F32),
            ve((3, PAIR, PATCH), F32), ve((4, n, PAIR), BF16), ve((2, PATCH, PAIR), BF16),
            ve((PAIR, PATCH), BF16), ve((PAIR, PATCH), BF16),
            ve((2, PATCH, PATCH), BF16), ve((3, PATCH, PAIR), BF16), ve((n, 512), BF16),
            ve((n, 512), F32), ve((n, 512), F32), ve((n, 128), F32), ve((4, n, PAIR), BF16),
            ve((4, 8 * rr, 512), BF16),
            ve((3, PATCH, PAIR), BF16), ve((2, PATCH, PAIR), F32), ve((2, PATCH, 512), F32),
            ve((n + PATCH // 2, 512), BF16), ve((n, 512), BF16),
            ve((3, 8 * rq, cols_q), BF16), ve((3, 4 * rq, cols_q), BF16), ve((3, 2 * rq, cols_q), BF16),
            ve((3, rq, cols_q), BF16), ve((2, rq, cols_q), BF16),
            ve((2, 4, 4 * rr, 256), BF16), ve((2, 4, 2 * rr, 256), BF16), ve((2, 4, rr, 256), BF16),
            ve((2, 3, rr, 256), BF16), ve((2, high, rr, 256), BF16), ve((high, rq, cols_q), BF16),
            ve((8, 16, 512), F32), ve((4, 16, 512), F32), ve((high + 1, 16, 512), F32),
            dma((2,)), dma((3,)), dma((copies,)), dma((copies,)), dma((2,)), dma((2,)), dma((3,)), dma((2, 4)),
            dma((5,)), dma((3,)), dma((2,)), dma((2,)),
        ],
        compiler_params=pltpu.CompilerParams(collective_id=0, has_side_effects=True, vmem_limit_bytes=VMEM_LIMIT),
    )(live, x, cot, wq, wk, wv, wo, up, down, vec)


def per_device(n_high, tokens, cotangent, norm1_gain, norm1_bias, query_weight, query_bias, key_weight,
               value_weight, value_bias, out_weight, out_bias, norm2_gain, norm2_bias, up_weight, up_bias,
               down_weight, down_bias, live_frames):
    m = lax.axis_index("mp")
    zero = jnp.zeros((512,), F32)
    heads = jnp.concatenate((query_bias.astype(F32), value_bias.astype(F32), jnp.zeros((256,), F32)))
    vec = jnp.stack([norm1_gain, norm1_bias, norm2_gain, norm2_bias, out_bias.astype(F32), down_bias.astype(F32),
                     zero, zero, heads, up_bias.astype(F32)] + [zero] * 6)
    layer_out, grad_tokens, fq, fr, fs, _ = layer(
        n_high, live_frames, tokens, cotangent, query_weight, key_weight, value_weight, out_weight, up_weight,
        down_weight, vec)
    fq = fq.astype(F32)
    fr = fr.astype(F32)
    gu = lax.dynamic_slice_in_dim(fs, 8 + m, 1, 0)[0]
    gqb = lax.dynamic_slice_in_dim(fs, 12 + m, 1, 0)[0]
    return (
        layer_out,
        grad_tokens,
        fs[0],
        fs[1],
        fq[:, :PAIR],
        gqb[:PAIR],
        fq[:, PAIR:2 * PAIR],
        fq[:, 2 * PAIR:],
        gqb[2 * PAIR:3 * PAIR],
        fr[0:PAIR],
        fs[4],
        fs[2],
        fs[3],
        fr[PAIR:PAIR + 512],
        gu,
        fr[PAIR + 512:],
        fs[5],
    )


def solution(mesh):
    rows, reps, cols = P(("dp", "mp"), None), P(), P(None, "mp")
    part, split = P("mp"), P("mp", None)
    in_specs = (rows, rows, reps, reps, cols, part, cols, cols, part, split, reps, reps, reps, cols, part,
                split, reps, P("dp"))
    out_specs = (rows, rows, reps, reps, cols, part, cols, cols, part, split, reps, reps, reps, cols, part,
                 split, reps)
    n_high = (mesh.shape["dp"] // 8).bit_length() - 1
    return jax.shard_map(
        functools.partial(per_device, n_high), mesh=mesh, in_specs=in_specs, out_specs=out_specs,
        check_vma=False,
    )
```

time: 1020 us -> 162 us (0.16)
  waiting for transfers between devices: 668 us -> 0 us
  matrix products: 185 us -> 0 us
  Pallas kernels: 0 us -> 143 us
  blocking collectives: 53.5 us -> 0 us
  local copies, waits for them, and re-layouts: 53.3 us -> 11.4 us
  other arithmetic: 33.6 us -> 3.37 us
  between operations: 15.6 us -> 1.33 us
    reduce_scatter x4 -> x0, waiting for transfers between devices: 385 us -> none  [the longest x1 111 us: per_device(): lax.psum_scatter(times_transposed(grad_projected, joined_weight), 'mp', s...]
    all_gather x4 -> x0, waiting for transfers between devices: 237 us -> none  [the longest x1 65.4 us: per_device(): lax.all_gather(normed_one.astype(jnp.bfloat16), 'mp', axis=0, tiled=True)]
    dot_general x33 -> x0, matrix products: 185 us -> none  [the longest x3 46.9 us: attend_back(): jnp.einsum('hqk,khd->qhd', grad_scores, key_heads, preferred_element_type...]
    pallas_call x0 -> x1, Pallas kernels: none -> 143 us  [layer(): pl.pallas_call(functools.partial(layer_kernel, n_high), name='layer', out...]
    psum x2 -> x0, blocking collectives: 53.5 us -> none  [the longest x1 40.5 us: per_device(): lax.psum((grad_norm1_gain, grad_norm1_bias, grad_norm2_gain, grad_norm2_b...]
    psum x1 -> x0, waiting for transfers between devices: 46.2 us -> none  [per_device(): lax.psum((grad_joined, grad_out, grad_up, grad_down, grad_joined_bias, gr...]
    reduce_sum x14 -> x0, other arithmetic: 23 us -> none  [the longest x3 6.14 us: normalize(): center = values - jnp.mean(values, axis=-1, keepdims=True)]
    while x20 -> x0, local copies, waits for them, and re-layouts: 19.8 us -> none  [the longest x4 10.5 us: per_device(): lax.map(attend_frame, (queries, key_heads, value_heads))]
  transfers between devices with their start and end apart: 9 -> 0, of which waited for: 9 -> 0; matrix products, arithmetic and copies ran while one was open for 4% -> 0% of each run, Pallas kernels for 0% -> 0%
where the time goes in v2:
time: 162 us; the launch traced here: 159 us
  Pallas kernels  143 us (88%)
  local copies, waits for them, and re-layouts  11.4 us (7%)
  other arithmetic  3.37 us (2%)
    pallas_call x1, Pallas kernels, layer(): pl.pallas_call(functools.partial(layer_kernel, n_high), name='layer', out...  143 us

profile of v2, /device:TPU:1, one launch (start us, length us, event | category | flops | bytes accessed | tf_op | source)
XLA Modules:
  0.0 159.0 jit_solution(14031934961818844676)
XLA Ops:
  1.3 0.7 stack.52
  2.0 0.7 stack.53
  2.7 0.7 convert_element_type.16
  3.3 0.7 convert_element_type.15
  4.0 0.7 stack.54
  4.7 2.0 %stack.51.vec_ref = f32[16,512]{1,0:T(8,128)} concatenate(f32[1,512]{1,0:T(1,128)} %bitcast.30, f32[1,512]{1,0:T(1,128)} %bitcast.31, f32[1,512]{1,0:T(1,128)} %bitcast.32, f32[1,512]{1,0:T(1,128)} %bitcast.33, f32[1,512]{1,0:T(1,128)S(1)} %bitcast.19, f32[1,512]{1,0:T(1,128)S(1)} %bitcast.20, f32[2,512]{1,0:T(2,128)S(1)} %broadcast.3, f32[1,512]{1,0:T(1,128)S(1)} %bitcast.21, ...), dimensions={0} | concatenate | bytes 65536 | tf_op jit(solution)/shard_map/stack | solution.py:794
  6.7 142.9 %layer.1 = (bf16[768,512]{1,0:T(8,128)(2,1)}, bf16[768,512]{1,0:T(8,128)(2,1)}, bf16[512,384]{1,0:T(8,128)(2,1)}, bf16[1152,512]{1,0:T(8,128)(2,1)}, f32[16,512]...) custom-call(s32[1]{0:T(128)S(6)} %copy.37.live_ref, bf16[768,512]{1,0:T(8,128)(2,1)} %x_ref.1, bf16[768,512]{1,0:T(8,128)(2,1)} %cot_ref.1, ...), custom_call_target="tpu_custom_call" | custom-call | tf_op jit(solution)/shard_map/layer/pallas_call | solution.py:753
  149.6 0.0 copy-start
  149.6 1.6 fusion.2
  151.2 1.9 %fusion.1 = (f32[512,128]{1,0:T(8,128)}, f32[512,128]{1,0:T(8,128)}, f32[512,128]{1,0:T(8,128)}) fusion(bf16[512,384]{1,0:T(8,128)(2,1)} %get-tuple-element.25), kind=kLoop, calls=%fused_computation.5 | loop fusion | bytes 1572864 | tf_op jit(solution)/shard_map/slice | solution.py:811
  153.1 1.3 dynamic-slice_bitcast_fusion
  154.4 0.0 copy-done
  154.4 0.7 slice.67
  155.1 0.0 copy-start.2
  155.1 1.6 %fusion = (f32[512,512]{1,0:T(8,128)}, f32[512,512]{1,0:T(8,128)}) fusion(bf16[1152,512]{1,0:T(8,128)(2,1)S(1)} %copy-done), kind=kLoop, calls=%fused_computation.4 | loop fusion | bytes 4194304 | tf_op jit(solution)/shard_map/slice | solution.py:819
  156.7 0.0 copy-start.1
  156.7 0.0 copy-done.2
  156.7 0.9 copy.38
  157.6 0.5 copy-done.1
  158.1 0.9 copy.39
  (4 shorter events, 0.0 us)
Async XLA Ops:
  149.6 4.8 %copy-start = (bf16[1152,512]{1,0:T(8,128)(2,1)S(1)}, bf16[1152,512]{1,0:T(8,128)(2,1)}, u32[]{:S(2)}) copy-start(bf16[1152,512]{1,0:T(8,128)(2,1)} %get-tuple-element.26) | copy-start | bytes 3538948
  155.1 1.6 %copy-start.2 = (bf16[768,512]{1,0:T(8,128)(2,1)S(1)}, bf16[768,512]{1,0:T(8,128)(2,1)}, u32[]{:S(2)}) copy-start(bf16[768,512]{1,0:T(8,128)(2,1)} %get-tuple-element.58) | copy-start | bytes 2359300
  156.7 1.4 copy-start.1

commit v3 on v2

--- a/solution.py
+++ b/solution.py
@@ -111,19 +111,21 @@
 FORWARD_CHUNKS = 2
 
 
-def layer_kernel(n_high, live_ref, x_ref, cot_ref, wq_ref, wk_ref, wv_ref, wo_ref, up_ref, down_ref, vec_ref,
-                 out_ref, gt_ref, oq_ref, or_ref, os_ref, p_ref,
-                 tok, ent_ref, gq_ref, gr_ref, gb_ref, qkv_ref, l_ref, ot_ref, mix_ref, kt_sc, qt_sc, vt_sc,
-                 p_sc, o_sc, e2_sc, res_sc, xhat_sc, rstd_sc, do_sc, dr_ref,
+def layer_kernel(n_high, live_ref, x_ref, cot_ref, wq_ref, wk_ref, wv_ref, wo_ref, up_ref, down_ref,
+                 n1g, n1b, n2g, n2b, bq, bv, b3,
+                 out_ref, gt_ref, oq_ref, oo_ref, ou_ref, os_ref, p_ref,
+                 vec_ref, tok, ent_ref, gq_ref, gr_ref, gb_ref, qkv_ref, l_ref, ot_ref, mix_ref, kt_sc, qt_sc, vt_sc,
+                 p_sc, o_sc, res_sc, xhat_sc, rstd_sc, do_sc, du_sc, dw_sc,
                  dot_in, dkv_sc, pn_sc, pnb_sc, got_sc,
-                 dq_sc, q3, q2, q1, qz, r3, r2, r1, rz, rh, qh, s_all, s_z, s_h,
+                 dq_sc, q4, qp, qz, w4, wp, wz, u3, u2, u1, uz, uh, qh, wh, s_all, s_z, s_h,
                  psem, lsem, send, recv, tsend, trecv, osend, orecv, dsend, drecv, bsend, brecv):
     d, m, core, lo, hi, flip_lo, flip_hi, flip_core = place()
     others = [(m + j) % 4 for j in (1, 2, 3)]
     froms = [(m + 3) % 4, (m + 2) % 4, (m + 1) % 4]
     cp = Copies(send, recv)
     base, at = (d // 8) * 8, d % 8
-    plane = [base + (at + j) % 8 for j in range(1, 8)]
+    near = [(at + j) % 8 for j in range(1, 8)]
+    plane = [base + o for o in near]
     highs = []
     for b in range(n_high):
         step = 8 * 2 ** b
@@ -144,6 +146,14 @@
     gq_ref[m, :, 0:PAIR] = wq_ref[...]
     gq_ref[m, :, PAIR:2 * PAIR] = wk_ref[...]
     gq_ref[m, :, 2 * PAIR:] = wv_ref[...]
+    vec_ref[...] = jnp.zeros_like(vec_ref)
+    for i, ref in enumerate((n1g, n1b, n2g, n2b)):
+        vec_ref[i:i + 1, :] = ref[...]
+    vec_ref[4:5, :] = b3[:, 0:512].astype(F32)
+    vec_ref[5:6, :] = b3[:, 512:1024].astype(F32)
+    vec_ref[8:9, 0:PAIR] = bq[...].astype(F32)
+    vec_ref[8:9, PAIR:2 * PAIR] = bv[...].astype(F32)
+    vec_ref[9:10, :] = b3[:, 1024:].astype(F32)
     gb_ref[m] = vec_ref[8:16, :]
 
     steps = ((flip_lo, piece, 1), (flip_hi, 4 * core + 2 * hi, 2), (flip_core, 4 * core, 4))
@@ -324,7 +334,7 @@
     e2t_sc = p_sc.at[0, pl.ds(0, 512), pl.ds(0, n_rows)]
     gf_sc[...] = (mask * cot_ref[...].astype(F32)).astype(BF16)
     os_ref[...] = jnp.zeros_like(os_ref)
-    os_ref[5:6, :] = jnp.sum(gf_sc[...].astype(F32), axis=0, keepdims=True)
+    os_ref[3:4, :] = jnp.sum(gf_sc[...].astype(F32), axis=0, keepdims=True)
     for k in range(4):
         @pl.when(m == k)
         def _():
@@ -355,7 +365,69 @@
     xhat_sc[...] = xhat
     rstd_sc[...] = jnp.broadcast_to(rstd, rstd_sc.shape)
 
-    def hidden(s, carry):
+    halves = (
+        (flip_core, 4 * (1 - core), 4 * core, 4),
+        (flip_hi, 4 * core + 2 * (1 - hi), 4 * core + 2 * hi, 2),
+        (flip_lo, 4 * core + 2 * hi + 1 - lo, piece, 1),
+    )
+    ru = du_sc.shape[1] // 8
+
+    class Flow:
+        def __init__(self, i):
+            self.i = i
+            self.half = [cp.make(du_sc.at[i, rows(away, n, ru), :], buf.at[i], (dev, m))
+                         for (dev, away, mine, n), buf in zip(halves, (u3, u2, u1))]
+            self.across = []
+            if i < 3:
+                self.across = [cp.make(du_sc.at[i, rows(piece, 1, ru), :], uz.at[i], (d, others[i]))]
+
+        def run(self, st):
+            i = self.i
+            if st > 0:
+                dev, away, mine, n = halves[st - 1]
+                buf = (u3, u2, u1)[st - 1]
+                self.half[st - 1].wait_recv()
+
+                def add(j, carry):
+                    sl = pl.ds(pl.multiple_of(mine * ru + j * ru, 16), ru)
+                    there = pl.ds(pl.multiple_of(j * ru, 16), ru)
+                    du_sc[i, sl, :] = du_sc[i, sl, :] + buf[i, there, :]
+                    return carry
+
+                lax.fori_loop(0, n, add, 0)
+            if st < 3:
+                self.half[st].start()
+            else:
+                start(self.across)
+
+    flows = [Flow(i) for i in range(4)]
+    parts = [ou_ref.at[rows(first, n, ru), :] for dev, first, n in steps]
+    double_u = [cp.make(part, part, (dev, m)) for part, (dev, first, n) in zip(parts, steps)]
+
+    def combine_u():
+        acc = du_sc[3, rows(piece, 1, ru), :].astype(F32)
+        for i in range(3):
+            flows[i].across[0].wait_recv()
+            acc += uz[i].astype(F32)
+        for b in range(n_high):
+            du_sc[3, rows(piece, 1, ru), :] = acc.astype(BF16)
+            cp.exchange(du_sc.at[3, rows(piece, 1, ru), :], uh.at[b], (highs[b], m))
+            acc += uh[b].astype(F32)
+        ou_ref[rows(piece, 1, ru), :] = acc.astype(BF16)
+        double_u[0].start()
+
+    def more_u(i):
+        double_u[i].wait_recv()
+        if i < 2:
+            double_u[i + 1].start()
+
+    hidden_schedule = {
+        2: lambda: flows[0].run(1),
+        3: lambda: (flows[0].run(2), flows[1].run(1)),
+    }
+
+    def hidden(i, carry):
+        s = (m + 1 + i) % 4
         up = gr_ref[s, PAIR:PAIR + 512, :]
         down = gr_ref[s, PAIR + 512:, :]
         pre = nn_dot(e2_in[...], up) + gb_ref[s, 1:2, :]
@@ -365,22 +437,30 @@
         act = (pre * half).astype(BF16)
         slope = half + (0.5 * GELU_C) * pre * (1.0 - th * th) * (1.0 + (3.0 * GELU_A) * sq)
         gp = (slope * nt_dot(gf_sc[...], down)).astype(BF16)
+        du_sc[i, 0:512, :] = nn_dot(e2t_sc[...], gp).astype(BF16)
+        du_sc[i, 512:, :] = tn_dot(act, gf_sc[...]).astype(BF16)
+        for k in range(4):
+            @pl.when(i == k)
+            def _():
+                flows[k].run(0)
         feed = nn_dot(act, down)
         gn = nt_dot(gp, up)
 
-        @pl.when(s == 0)
+        @pl.when(i == 0)
         def _():
             pn_sc[0, 0:n_rows, :] = feed
             pn_sc[1, 0:n_rows, :] = gn
 
-        @pl.when(s > 0)
+        @pl.when(i > 0)
         def _():
             pn_sc[0, 0:n_rows, :] += feed
             pn_sc[1, 0:n_rows, :] += gn
 
-        dr_ref[s, PAIR:PAIR + 512, :] = nn_dot(e2t_sc[...], gp).astype(BF16)
-        dr_ref[s, PAIR + 512:, :] = tn_dot(act, gf_sc[...]).astype(BF16)
-        os_ref[pl.ds(8 + s, 1), :] = jnp.sum(gp.astype(F32), axis=0, keepdims=True)
+        os_ref[pl.ds(4 + s, 1), :] = jnp.sum(gp.astype(F32), axis=0, keepdims=True)
+        for k in hidden_schedule:
+            @pl.when(i == k)
+            def _():
+                hidden_schedule[k]()
         return carry
 
     lax.fori_loop(0, 4, hidden, 0)
@@ -431,98 +511,109 @@
     for h in range(2):
         fetch(order[0], h).start()
 
-    halves = (
-        (flip_core, 4 * (1 - core), 4 * core, 4),
-        (flip_hi, 4 * core + 2 * (1 - hi), 4 * core + 2 * hi, 2),
-        (flip_lo, 4 * core + 2 * hi + 1 - lo, piece, 1),
-    )
-
-    class Flow:
-        def __init__(self, c):
-            self.c, self.lanes = c, slice(256 * c, 256 * c + 256)
-            cols = pl.ds(256 * c, 256)
-            self.half = [cp.make(dr_ref.at[:, rows(away, n, rr), cols], buf.at[c], (dev, m))
-                         for (dev, away, mine, n), buf in zip(halves, (r3, r2, r1))]
-            self.across = [cp.make(dr_ref.at[others[j], rows(piece, 1, rr), cols], rz.at[c, j], (d, others[j]))
-                           for j in range(3)]
-            parts = [or_ref.at[rows(first, n, rr), cols] for dev, first, n in steps]
-            self.double = [cp.make(part, part, (dev, m)) for part, (dev, first, n) in zip(parts, steps)]
+    flip_both = flip_lo + flip_hi - d
+    same_core = ((flip_lo, 4 * core + 2 * hi + 1 - lo), (flip_hi, 4 * core + 2 * (1 - hi) + lo),
+                 (flip_both, 4 * core + 2 * (1 - hi) + 1 - lo))
+
+    class Hops:
+        def __init__(self, part, four, three, across):
+            self.part, self.four, self.three = part, four, three
+            self.core = cp.make(part(4 * (1 - core), 4), four, (flip_core, m))
+            self.plane = [cp.make(part(p, 1), three.at[j], (dev, m)) for j, (dev, p) in enumerate(same_core)]
+            self.across = [cp.make(*c) for c in across]
 
         def run(self, st):
-            c, lanes = self.c, self.lanes
             if st == 0:
-                self.half[0].start()
-            elif st <= 3:
-                dev, away, mine, n = halves[st - 1]
-                buf = (r3, r2, r1)[st - 1]
-                self.half[st - 1].wait_recv()
-
-                def add(s, carry):
-                    sl = rows(mine, n, rr)
-                    dr_ref[s, sl, lanes] = (dr_ref[s, sl, lanes].astype(F32) + buf[c, s].astype(F32)).astype(BF16)
-                    return carry
-
-                lax.fori_loop(0, 4, add, 0)
-                if st < 3:
-                    self.half[st].start()
-                else:
-                    start(self.across)
-            elif st == 4:
-                acc = dr_ref[m, rows(piece, 1, rr), lanes].astype(F32)
+                self.core.start()
+            elif st == 1:
+                self.core.wait_recv()
+                mine = self.part(4 * core, 4)
+                mine[...] = mine[...] + self.four[...]
+                start(self.plane)
+            else:
+                acc = self.part(piece, 1)[...].astype(F32)
+                for j in range(3):
+                    self.plane[j].wait_recv()
+                    acc += self.three[j].astype(F32)
+                self.part(piece, 1)[...] = acc.astype(BF16)
+                start(self.across)
+
+    class Spread:
+        def __init__(self, part):
+            one, half = part(piece, 1), part(4 * core, 4)
+            self.plane = [cp.make(one, one, (dev, m)) for dev, p in same_core]
+            self.core = cp.make(half, half, (flip_core, m))
+
+        def run(self, st):
+            if st == 0:
+                start(self.plane)
+            elif st == 1:
+                arrive(self.plane)
+                self.core.start()
+            else:
+                self.core.wait_recv()
+
+    rw = dw_sc.shape[1] // 8
+
+    def task_part(t):
+        return lambda p, n: dq_sc.at[t, rows(p, n, rq), :]
+
+    def out_part(p, n):
+        return dw_sc.at[:, rows(p, n, rw), :]
+
+    heads = [Hops(task_part(t), q4.at[t], qp.at[t],
+                  [(task_part(t)(piece, 1), qz.at[t - 1], (d, shards[t]))] if t > 0 else [])
+             for t in range(3)]
+    outs = Hops(out_part, w4, wp, [(dw_sc.at[others[j], rows(piece, 1, rw), :], wz.at[j], (d, others[j]))
+                                   for j in range(3)])
+
+    class Small:
+        def __init__(self, g):
+            self.g, self.rows = g, slice(8 * g, 8 * g + 8)
+            self.plane = [cp.make(s_all.at[g, 7], s_all.at[g, j], (plane[j], m)) for j in range(7)]
+            self.across = [cp.make(s_z.at[g, 3], s_z.at[g, j], (d, others[j])) for j in range(3)]
+
+        def run(self, st):
+            g = self.g
+            if st == 0:
+                s_all[g, 7] = os_ref[self.rows, :]
+                start(self.plane)
+            elif st == 1:
+                acc = s_all[g, 7]
+                for j in range(7):
+                    self.plane[j].wait_recv()
+                    acc += s_all[g, j]
+                s_z[g, 3] = acc
+                start(self.across)
+            else:
+                acc = s_z[g, 3]
                 for j in range(3):
                     self.across[j].wait_recv()
-                    acc += rz[c, j].astype(F32)
+                    acc += s_z[g, j]
                 for b in range(n_high):
-                    dr_ref[m, rows(piece, 1, rr), lanes] = acc.astype(BF16)
-                    cp.exchange(dr_ref.at[m, rows(piece, 1, rr), pl.ds(256 * c, 256)], rh.at[c, b], (highs[b], m))
-                    acc += rh[c, b].astype(F32)
-                or_ref[rows(piece, 1, rr), lanes] = acc.astype(BF16)
-                self.double[0].start()
-            elif st <= 6:
-                self.double[st - 5].wait_recv()
-                self.double[st - 4].start()
-            else:
-                self.double[2].wait_recv()
-
-    class HeadFlow:
-        def __init__(self, t):
-            self.t = t
-            self.half = [cp.make(dq_sc.at[t, rows(away, n, rq), :], buf.at[t], (dev, m))
-                         for (dev, away, mine, n), buf in zip(halves, (q3, q2, q1))]
-            self.across = []
-            if t > 0:
-                self.across = [cp.make(dq_sc.at[t, rows(piece, 1, rq), :], qz.at[t - 1], (d, shards[t]))]
-
-        def run(self, st):
-            t = self.t
-            if st > 0:
-                dev, away, mine, n = halves[st - 1]
-                self.half[st - 1].wait_recv()
-                sl = rows(mine, n, rq)
-                buf = (q3, q2, q1)[st - 1]
-                dq_sc[t, sl, :] = (dq_sc[t, sl, :].astype(F32) + buf[t].astype(F32)).astype(BF16)
-            if st < 3:
-                self.half[st].start()
-            else:
-                start(self.across)
-
-    flows = [Flow(0), Flow(1)]
-    heads = [HeadFlow(t) for t in range(3)]
+                    s_h[g, 0] = acc
+                    cp.exchange(s_h.at[g, 0], s_h.at[g, 1 + b], (highs[b], m))
+                    acc += s_h[g, 1 + b]
+                os_ref[self.rows, :] = acc
+
+    early, late = Small(0), Small(1)
+
+    flows[0].run(3)
+    flows[1].run(2)
+    flows[2].run(1)
     gw = tn_dot(mix, ga).astype(BF16)
     for s in range(4):
-        dr_ref[s, 0:PAIR, :] = gw[s * PAIR:(s + 1) * PAIR, :]
-    flows[0].run(0)
-    flows[1].run(0)
-    os_ref[2:3, :] = jnp.sum(gn * xhat, axis=0, keepdims=True)
-    os_ref[3:4, :] = jnp.sum(gn, axis=0, keepdims=True)
-    os_ref[4:5, :] = jnp.sum(ga.astype(F32), axis=0, keepdims=True)
+        dw_sc[s] = gw[s * PAIR:(s + 1) * PAIR, :]
+    outs.run(0)
+    os_ref[0:1, :] = jnp.sum(gn * xhat, axis=0, keepdims=True)
+    os_ref[1:2, :] = jnp.sum(gn, axis=0, keepdims=True)
+    os_ref[2:3, :] = jnp.sum(ga.astype(F32), axis=0, keepdims=True)
+    early.run(0)
     out_ref[...] = (mask * (res_sc[...] + pn_sc[0, 0:n_rows, :] + vec_ref[5:6, :])).astype(BF16)
     res_sc[...] = gres
-    for k in range(4):
-        @pl.when(m == k)
-        def _():
-            for ls, n, slot, fs, other in SEGMENTS[k]:
-                e2_sc[ls:ls + n, :] = tok[slot, fs:fs + n, :]
+    flows[1].run(3)
+    flows[2].run(2)
+    flows[3].run(1)
 
     def first_stats(i, carry):
         rs = pl.ds(pl.multiple_of(i * 256, 256), 256)
@@ -533,7 +624,21 @@
         return carry
 
     lax.fori_loop(0, n_rows // 256, first_stats, 0)
-    flows[0].run(1)
+
+    spread_w = Spread(lambda p, n: oo_ref.at[rows(p, n, rw), :])
+    spread_q = Spread(lambda p, n: oq_ref.at[rows(p, n, rq), :])
+
+    def combine_w():
+        acc = dw_sc[m, rows(piece, 1, rw), :].astype(F32)
+        for j in range(3):
+            outs.across[j].wait_recv()
+            acc += wz[j].astype(F32)
+        for b in range(n_high):
+            dw_sc[m, rows(piece, 1, rw), :] = acc.astype(BF16)
+            cp.exchange(dw_sc.at[m, rows(piece, 1, rw), :], wh.at[b], (highs[b], m))
+            acc += wh[b].astype(F32)
+        oo_ref[rows(piece, 1, rw), :] = acc.astype(BF16)
+        spread_w.run(0)
 
     def row_copy(k, i):
         ls, n, slot, fs, other = SEGMENTS[k][i]
@@ -552,18 +657,19 @@
 
         zero = jnp.zeros((1, 512), F32)
         gain_sum, bias_sum = lax.fori_loop(0, PATCH // 256, block, (zero, zero))
-        os_ref[0:1, :] += gain_sum
-        os_ref[1:2, :] += bias_sum
+        os_ref[8:9, :] += gain_sum
+        os_ref[9:10, :] += bias_sum
 
     back_schedule = {
-        (0, 1): lambda: flows[1].run(1),
-        (0, 2): lambda: flows[0].run(2),
-        (1, 0): lambda: flows[1].run(2),
-        (1, 1): lambda: (flows[0].run(3), heads[2].run(1)),
-        (1, 2): lambda: (flows[1].run(3), heads[2].run(2)),
-        (2, 0): lambda: flows[0].run(4),
-        (2, 1): lambda: (heads[2].run(3), heads[0].run(1)),
-        (2, 2): lambda: (flows[1].run(4), heads[0].run(2), flows[0].run(5)),
+        (0, 0): lambda: (flows[2].run(3), flows[3].run(2), outs.run(1)),
+        (0, 1): lambda: (flows[3].run(3), early.run(1)),
+        (0, 2): lambda: outs.run(2),
+        (1, 0): lambda: combine_u(),
+        (1, 1): lambda: (heads[2].run(1), early.run(2), more_u(0)),
+        (1, 2): lambda: (heads[2].run(2), combine_w()),
+        (2, 0): lambda: more_u(1),
+        (2, 1): lambda: (heads[0].run(1), spread_w.run(1)),
+        (2, 2): lambda: (heads[0].run(2), more_u(2)),
     }
     width = 256
 
@@ -666,34 +772,18 @@
         return carry
 
     lax.fori_loop(0, 3, back_task, 0)
-    s_all[7] = os_ref[...]
-    wave = [cp.push(s_all.at[7], s_all.at[j], (plane[j], m)) for j in range(7)]
-    flows[1].run(5)
-    flows[0].run(6)
-    heads[0].run(3)
+    late.run(0)
     heads[1].run(1)
-    acc = os_ref[...]
-    for j in range(7):
-        wave[j].wait_recv()
-        acc += s_all[j]
-    s_z[3] = acc
-    wave = [cp.push(s_z.at[3], s_z.at[j], (d, others[j])) for j in range(3)]
+    xn_sc = p_sc.at[0, pl.ds(0, n_rows), pl.ds(0, 512)]
+    for k in range(4):
+        @pl.when(m == k)
+        def _():
+            for ls, n, slot, fs, other in SEGMENTS[k]:
+                xn_sc[ls:ls + n, :] = tok[slot, fs:fs + n, :]
+    late.run(1)
     heads[1].run(2)
-    flows[1].run(6)
-    flows[0].run(7)
-    heads[1].run(3)
-    flows[1].run(7)
-    for j in range(3):
-        wave[j].wait_recv()
-        acc += s_z[j]
-    for b in range(n_high):
-        s_h[0] = acc
-        cp.exchange(s_h.at[0], s_h.at[1 + b], (highs[b], m))
-        acc += s_h[1 + b]
-    os_ref[...] = acc
-
     acc = dq_sc[0, rows(piece, 1, rq), :].astype(F32)
-    for t in (1, 2):
+    for t in (2, 1):
         heads[t].across[0].wait_recv()
         acc += qz[t - 1].astype(F32)
     for b in range(n_high):
@@ -701,14 +791,9 @@
         cp.exchange(dq_sc.at[0, rows(piece, 1, rq), :], qh.at[b], (highs[b], m))
         acc += qh[b].astype(F32)
     oq_ref[rows(piece, 1, rq), :] = acc.astype(BF16)
-
-    def double_q(i):
-        dev, first, n = steps[i]
-        part = oq_ref.at[rows(first, n, rq), :]
-        return cp.push(part, part, (dev, m))
-
-    qw = double_q(0)
-
+    spread_q.run(0)
+
+    spread_q.run(1)
     for k in range(4):
         @pl.when(m == k)
         def _():
@@ -719,15 +804,14 @@
     for r in range(0, n_rows, 256):
         rs = slice(r, r + 256)
         gn = xhat_sc[rs, :] + got_sc[rs, :].astype(F32)
-        xhat = e2_sc[rs, :].astype(F32)
+        xhat = xn_sc[rs, :].astype(F32)
         gg = gn * vec_ref[0:1, :]
         mg = jnp.mean(gg, axis=-1, keepdims=True)
         mx = jnp.mean(gg * xhat, axis=-1, keepdims=True)
         gt_ref[rs, :] = (res_sc[rs, :] + rstd_sc[rs, 0:1] * (gg - mg - xhat * mx)).astype(BF16)
-        if r < 512:
-            qw.wait_recv()
-            qw = double_q(1 + r // 256)
-    qw.wait_recv()
+    late.run(2)
+    spread_q.run(2)
+    spread_w.run(2)
     for k in range(4):
         @pl.when(m == k)
         def _():
@@ -741,13 +825,14 @@
     cp.finish()
 
 
-def layer(n_high, live, x, cot, wq, wk, wv, wo, up, down, vec):
+def layer(n_high, live, x, cot, wq, wk, wv, wo, up, down, *vectors):
     dma = pltpu.SemaphoreType.DMA
     n = x.shape[0]
-    cols_q, rows_r = 3 * PAIR, wo.shape[0] + up.shape[0] + down.shape[0]
-    rq, rr = wq.shape[0] // 8, rows_r // 8
+    cols_q, rows_u = 3 * PAIR, up.shape[0] + down.shape[0]
+    rows_o = wo.shape[0]
+    rq, ro, ru = wq.shape[0] // 8, rows_o // 8, rows_u // 8
     high = max(n_high, 1)
-    copies = 11 + FORWARD_CHUNKS * 12 + 2 * (9 + n_high) + 11 + 10 + 3 + 2 * n_high
+    copies = 11 + FORWARD_CHUNKS * 12 + 18 + 14 + 7 + 20 + 8 + 5 * n_high
     vmem = pl.BlockSpec(memory_space=pltpu.VMEM)
     ve = pltpu.VMEM
     return pl.pallas_call(
@@ -757,68 +842,95 @@
             jax.ShapeDtypeStruct((n, 512), BF16),
             jax.ShapeDtypeStruct((n, 512), BF16),
             jax.ShapeDtypeStruct((8 * rq, cols_q), BF16),
-            jax.ShapeDtypeStruct((8 * rr, 512), BF16),
+            jax.ShapeDtypeStruct((rows_o, 512), BF16),
+            jax.ShapeDtypeStruct((rows_u, 512), BF16),
             jax.ShapeDtypeStruct((16, 512), F32),
             jax.ShapeDtypeStruct((3, 2, PATCH, PATCH), BF16),
         ),
-        in_specs=[pl.BlockSpec(memory_space=pltpu.SMEM)] + [vmem] * 9,
-        out_specs=(vmem,) * 5 + (ANY,),
+        in_specs=[pl.BlockSpec(memory_space=pltpu.SMEM)] + [vmem] * 15,
+        out_specs=(vmem,) * 6 + (ANY,),
         scratch_shapes=[
+            ve((16, 512), F32),
             ve((2, PATCH, 512), BF16), ve((2, PATCH, 512), BF16), ve((4, 8 * rq, cols_q), BF16),
-            ve((4, 8 * rr, 512), BF16), ve((4, 8, 512), F32), ve((3, PATCH, cols_q), BF16), ve((3, 8, PATCH), F32),
-            ve((3, PAIR, PATCH), F32), ve((4, n, PAIR), BF16), ve((2, PATCH, PAIR), BF16),
+            ve((4, rows_o + rows_u, 512), BF16), ve((4, 8, 512), F32), ve((3, PATCH, cols_q), BF16),
+            ve((3, 8, PATCH), F32), ve((3, PAIR, PATCH), F32), ve((4, n, PAIR), BF16), ve((2, PATCH, PAIR), BF16),
             ve((PAIR, PATCH), BF16), ve((PAIR, PATCH), BF16),
-            ve((2, PATCH, PATCH), BF16), ve((3, PATCH, PAIR), BF16), ve((n, 512), BF16),
+            ve((2, PATCH, PATCH), BF16), ve((3, PATCH, PAIR), BF16),
             ve((n, 512), F32), ve((n, 512), F32), ve((n, 128), F32), ve((4, n, PAIR), BF16),
-            ve((4, 8 * rr, 512), BF16),
+            ve((4, rows_u, 512), BF16), ve((4, rows_o, 512), BF16),
             ve((3, PATCH, PAIR), BF16), ve((2, PATCH, PAIR), F32), ve((2, PATCH, 512), F32),
             ve((n + PATCH // 2, 512), BF16), ve((n, 512), BF16),
-            ve((3, 8 * rq, cols_q), BF16), ve((3, 4 * rq, cols_q), BF16), ve((3, 2 * rq, cols_q), BF16),
-            ve((3, rq, cols_q), BF16), ve((2, rq, cols_q), BF16),
-            ve((2, 4, 4 * rr, 256), BF16), ve((2, 4, 2 * rr, 256), BF16), ve((2, 4, rr, 256), BF16),
-            ve((2, 3, rr, 256), BF16), ve((2, high, rr, 256), BF16), ve((high, rq, cols_q), BF16),
-            ve((8, 16, 512), F32), ve((4, 16, 512), F32), ve((high + 1, 16, 512), F32),
+            ve((3, 8 * rq, cols_q), BF16), ve((3, 4 * rq, cols_q), BF16), ve((3, 3, rq, cols_q), BF16), ve((2, rq, cols_q), BF16),
+            ve((4, 4 * ro, 512), BF16), ve((3, 4, ro, 512), BF16), ve((3, ro, 512), BF16),
+            ve((4, 4 * ru, 512), BF16), ve((4, 2 * ru, 512), BF16), ve((4, ru, 512), BF16), ve((3, ru, 512), BF16),
+            ve((high, ru, 512), BF16), ve((high, rq, cols_q), BF16), ve((high, ro, 512), BF16),
+            ve((2, 8, 8, 512), F32), ve((2, 4, 8, 512), F32), ve((2, high + 1, 8, 512), F32),
             dma((2,)), dma((3,)), dma((copies,)), dma((copies,)), dma((2,)), dma((2,)), dma((3,)), dma((2, 4)),
             dma((5,)), dma((3,)), dma((2,)), dma((2,)),
         ],
         compiler_params=pltpu.CompilerParams(collective_id=0, has_side_effects=True, vmem_limit_bytes=VMEM_LIMIT),
-    )(live, x, cot, wq, wk, wv, wo, up, down, vec)
+    )(live, x, cot, wq, wk, wv, wo, up, down, *[v.reshape(1, -1) for v in vectors])
+
+
+def unpack_kernel(pick_ref, out_ref, gt_ref, q_ref, o_ref, up_ref, down_ref, s_ref,
+                  out, gt, gq, gk, gv, go, gu, gd, n1g, n1b, n2g, n2b, bo, bd, bu, bq, bv):
+    out[...] = out_ref[...]
+    gt[...] = gt_ref[...]
+    gq[...] = q_ref[:, 0:PAIR].astype(F32)
+    gk[...] = q_ref[:, PAIR:2 * PAIR].astype(F32)
+    gv[...] = q_ref[:, 2 * PAIR:].astype(F32)
+    go[...] = o_ref[...].astype(F32)
+    gu[...] = up_ref[...].astype(F32)
+    gd[...] = down_ref[...].astype(F32)
+    m = pick_ref[0]
+    for r, ref in ((8, n1g), (9, n1b), (0, n2g), (1, n2b), (2, bo), (3, bd)):
+        ref[...] = s_ref[r:r + 1, :]
+    bu[...] = s_ref[pl.ds(4 + m, 1), :]
+    heads = s_ref[pl.ds(12 + m, 1), :]
+    bq[...] = heads[:, 0:PAIR]
+    bv[...] = heads[:, 2 * PAIR:3 * PAIR]
+
+
+def unpack(pick, out, gt, q, o, u, s):
+    steps = 4
+    n, rq, ro, ru = out.shape[0] // steps, q.shape[0] // steps, o.shape[0] // steps, u.shape[0] // (2 * steps)
+
+    def block(r, c):
+        return pl.BlockSpec((r, c), lambda i: (i, 0))
+
+    def whole(r, c):
+        return pl.BlockSpec((r, c), lambda i: (0, 0))
+
+    f32 = functools.partial(jax.ShapeDtypeStruct, dtype=F32)
+    return pl.pallas_call(
+        unpack_kernel,
+        name="unpack",
+        grid=(steps,),
+        out_shape=(
+            jax.ShapeDtypeStruct(out.shape, BF16), jax.ShapeDtypeStruct(gt.shape, BF16),
+            f32((q.shape[0], PAIR)), f32((q.shape[0], PAIR)), f32((q.shape[0], PAIR)), f32(o.shape),
+            f32((u.shape[0] // 2, 512)), f32((u.shape[0] // 2, 512)),
+        ) + (f32((1, 512)),) * 7 + (f32((1, PAIR)),) * 2,
+        in_specs=[pl.BlockSpec(memory_space=pltpu.SMEM), block(n, 512), block(n, 512), block(rq, q.shape[1]),
+                  block(ro, 512), block(ru, 512), pl.BlockSpec((ru, 512), lambda i: (i + steps, 0)),
+                  whole(*s.shape)],
+        out_specs=(block(n, 512), block(n, 512), block(rq, PAIR), block(rq, PAIR), block(rq, PAIR), block(ro, 512),
+                   block(ru, 512), block(ru, 512)) + (whole(1, 512),) * 7 + (whole(1, PAIR),) * 2,
+        compiler_params=pltpu.CompilerParams(vmem_limit_bytes=60 << 20),
+    )(pick, out, gt, q, o, u, u, s)
 
 
 def per_device(n_high, tokens, cotangent, norm1_gain, norm1_bias, query_weight, query_bias, key_weight,
                value_weight, value_bias, out_weight, out_bias, norm2_gain, norm2_bias, up_weight, up_bias,
                down_weight, down_bias, live_frames):
-    m = lax.axis_index("mp")
-    zero = jnp.zeros((512,), F32)
-    heads = jnp.concatenate((query_bias.astype(F32), value_bias.astype(F32), jnp.zeros((256,), F32)))
-    vec = jnp.stack([norm1_gain, norm1_bias, norm2_gain, norm2_bias, out_bias.astype(F32), down_bias.astype(F32),
-                     zero, zero, heads, up_bias.astype(F32)] + [zero] * 6)
-    layer_out, grad_tokens, fq, fr, fs, _ = layer(
+    packed = layer(
         n_high, live_frames, tokens, cotangent, query_weight, key_weight, value_weight, out_weight, up_weight,
-        down_weight, vec)
-    fq = fq.astype(F32)
-    fr = fr.astype(F32)
-    gu = lax.dynamic_slice_in_dim(fs, 8 + m, 1, 0)[0]
-    gqb = lax.dynamic_slice_in_dim(fs, 12 + m, 1, 0)[0]
-    return (
-        layer_out,
-        grad_tokens,
-        fs[0],
-        fs[1],
-        fq[:, :PAIR],
-        gqb[:PAIR],
-        fq[:, PAIR:2 * PAIR],
-        fq[:, 2 * PAIR:],
-        gqb[2 * PAIR:3 * PAIR],
-        fr[0:PAIR],
-        fs[4],
-        fs[2],
-        fs[3],
-        fr[PAIR:PAIR + 512],
-        gu,
-        fr[PAIR + 512:],
-        fs[5],
-    )
+        down_weight, norm1_gain, norm1_bias, norm2_gain, norm2_bias, query_bias, value_bias,
+        jnp.concatenate((out_bias, down_bias, up_bias)))
+    pick = lax.axis_index("mp").astype(jnp.int32).reshape(1)
+    out, gt, gq, gk, gv, go, gu, gd, *sums = unpack(pick, *packed[:6])
+    n1g, n1b, n2g, n2b, bo, bd, bu, bq, bv = [v.reshape(-1) for v in sums]
+    return (out, gt, n1g, n1b, gq, bq, gk, gv, bv, go, bo, n2g, n2b, gu, bu, gd, bd)
 
 
 def solution(mesh):

time: 162 us -> 146 us (0.901); the launches traced: 159 us -> 146 us
  local copies, waits for them, and re-layouts: 11.4 us -> 0.6 us
  other arithmetic: 3.37 us -> 0.72 us
    slice x5 -> x0, local copies, waits for them, and re-layouts: 7.08 us -> none  [the longest x1 1.92 us: per_device(): fq[:, 2 * PAIR:]]
    pallas_call x0 -> x1, Pallas kernels: none -> 4.68 us  [unpack(): pl.pallas_call(unpack_kernel, name='unpack', grid=(steps,), out_shape=(ja...]
    pallas_call x1, Pallas kernels: 143 us -> 139 us  [layer(): pl.pallas_call(functools.partial(layer_kernel, n_high), name='layer', out...]
    unnamed x8 -> x0, local copies, waits for them, and re-layouts: 2.3 us -> none
    another operation x3 -> x0, other arithmetic: 2.04 us -> none  [per_device(): jnp.stack([norm1_gain, norm1_bias, norm2_gain, norm2_bias, out_bias.astyp...]
    another operation x3 -> x0, local copies, waits for them, and re-layouts: 1.98 us -> none  [the longest x2 1.98 us: per_device(): jnp.stack([norm1_gain, norm1_bias, norm2_gain, norm2_bias, out_bias.astyp...]
where the time goes in v3:
time: 146 us
  Pallas kernels  143 us (98%)
  between operations  1.49 us (1%)
    pallas_call x1, Pallas kernels, layer(): pl.pallas_call(functools.partial(layer_kernel, n_high), name='layer', out...  139 us
    pallas_call x1, Pallas kernels, unpack(): pl.pallas_call(unpack_kernel, name='unpack', grid=(steps,), out_shape=(ja...  4.68 us

profile of v3, /device:TPU:1, one launch (start us, length us, event | category | flops | bytes accessed | tf_op | source)
XLA Modules:
  0.0 146.1 jit_solution(6772946110458209101)
XLA Ops:
  0.7 0.7 pad_maximum_fusion
  1.4 0.6 reshape.92.b3
  2.6 138.6 %layer.1 = (bf16[768,512]{1,0:T(8,128)(2,1)}, bf16[768,512]{1,0:T(8,128)(2,1)}, bf16[512,384]{1,0:T(8,128)(2,1)}, bf16[128,512]{1,0:T(8,128)(2,1)}, bf16[1024,51...) custom-call(s32[1]{0:T(128)S(6)} %copy.35.live_ref, bf16[768,512]{1,0:T(8,128)(2,1)} %x_ref.1, ...), custom_call_target="tpu_custom_call" | custom-call | tf_op jit(solution)/shard_map/layer/pallas_call | solution.py:838
  141.2 4.7 %unpack.1 = (bf16[768,512]{1,0:T(8,128)(2,1)}, bf16[768,512]{1,0:T(8,128)(2,1)}, f32[512,128]{1,0:T(8,128)}, f32[512,128]{1,0:T(8,128)}, f32[512,128]{1,0:T(8,12...) custom-call(s32[1]{0:T(128)} %bitcast.pick_ref, ...), custom_call_target="tpu_custom_call" | custom-call | tf_op jit(solution)/shard_map/unpack/pallas_call | solution.py:905

commit v4 on v3

--- a/solution.py
+++ b/solution.py
@@ -60,13 +60,6 @@
     return d, m, core, lo, hi, flip_lo, flip_hi, flip_core
 
 
-def barrier(targets):
-    sem = pltpu.get_barrier_semaphore()
-    for dev in targets:
-        pl.semaphore_signal(sem, inc=1, device_id=dev, device_id_type=MESH)
-    pl.semaphore_wait(sem, len(targets))
-
-
 VMEM_LIMIT = 63 << 20
 
 
@@ -108,17 +101,14 @@
         c.wait_recv()
 
 
-FORWARD_CHUNKS = 2
-
-
-def layer_kernel(n_high, live_ref, x_ref, cot_ref, wq_ref, wk_ref, wv_ref, wo_ref, up_ref, down_ref,
+def layer_kernel(n_high, live_ref, x_hbm, cot_hbm, wq_ref, wk_ref, wv_ref, wo_ref, up_ref, down_ref,
                  n1g, n1b, n2g, n2b, bq, bv, b3,
-                 out_ref, gt_ref, oq_ref, oo_ref, ou_ref, os_ref, p_ref,
-                 vec_ref, tok, ent_ref, gq_ref, gr_ref, gb_ref, qkv_ref, l_ref, ot_ref, mix_ref, kt_sc, qt_sc, vt_sc,
+                 out_hbm, gt_ref, oq_ref, oo_ref, ou_ref, os_ref, p_ref,
+                 x_ref, cot_ref, out_ref, vec_ref, tok, ent_ref, gq_ref, gr_ref, gb_ref, qkv_ref, l_ref, ot_ref, mix_ref, kt_sc, qt_sc, vt_sc,
                  p_sc, o_sc, res_sc, xhat_sc, rstd_sc, do_sc, du_sc, dw_sc,
                  dot_in, dkv_sc, pn_sc, pnb_sc, got_sc,
                  dq_sc, q4, qp, qz, w4, wp, wz, u3, u2, u1, uz, uh, qh, wh, s_all, s_z, s_h,
-                 psem, lsem, send, recv, tsend, trecv, osend, orecv, dsend, drecv, bsend, brecv):
+                 psem, lsem, isem, wsem, outsem, send, recv, tsend, trecv, osend, orecv, dsend, drecv, bsend, brecv):
     d, m, core, lo, hi, flip_lo, flip_hi, flip_core = place()
     others = [(m + j) % 4 for j in (1, 2, 3)]
     froms = [(m + 3) % 4, (m + 2) % 4, (m + 1) % 4]
@@ -140,9 +130,20 @@
     def rows(first, n, size):
         return pl.ds(pl.multiple_of(first * size, 16), n * size)
 
-    gr_ref[m, 0:n_out, :] = wo_ref[...]
-    gr_ref[m, n_out:n_out + n_up, :] = up_ref[...]
-    gr_ref[m, n_out + n_up:, :] = down_ref[...]
+    partners = [(d, o) for o in others] + [(o, m) for o in plane] + [(h, m) for h in highs]
+    entry = pltpu.get_barrier_semaphore()
+    for dev in partners:
+        pl.semaphore_signal(entry, inc=1, device_id=dev, device_id_type=MESH)
+    x_copy = pltpu.make_async_copy(x_hbm, x_ref, isem.at[0])
+    cot_copy = pltpu.make_async_copy(cot_hbm, cot_ref, isem.at[1])
+    own = [
+        pltpu.make_async_copy(wo_ref, gr_ref.at[m, pl.ds(0, n_out), :], wsem.at[0]),
+        pltpu.make_async_copy(up_ref, gr_ref.at[m, pl.ds(n_out, n_up), :], wsem.at[1]),
+        pltpu.make_async_copy(down_ref, gr_ref.at[m, pl.ds(n_out + n_up, down_ref.shape[0]), :], wsem.at[2]),
+    ]
+    x_copy.start()
+    start(own)
+    cot_copy.start()
     gq_ref[m, :, 0:PAIR] = wq_ref[...]
     gq_ref[m, :, PAIR:2 * PAIR] = wk_ref[...]
     gq_ref[m, :, 2 * PAIR:] = wv_ref[...]
@@ -158,20 +159,25 @@
 
     steps = ((flip_lo, piece, 1), (flip_hi, 4 * core + 2 * hi, 2), (flip_core, 4 * core, 4))
     part = gq_ref.at[m, rows(piece, 1, rq), :]
-    waves_q = [[cp.make(part, part, (d, dev)) for dev in (second, third)]]
+    ro = n_out // 8
+    far = [(m + 3 - u) % 4 for u in range(3)]
+    near_shard = [(m + 1 + u) % 4 for u in range(3)]
+    out_rows = gr_ref.at[m, rows(piece, 1, ro), :]
+    waves_q = [[cp.make(part, part, (d, dev)) for dev in (second, third)]
+               + [cp.make(out_rows, out_rows, (d, dev)) for dev in far]]
     waves_b = [cp.make(vec_ref.at[pl.ds(8, 8), :], gb_ref.at[m], (d, o)) for o in others]
     for dev, first, n in steps:
         parts = [gq_ref.at[sh, rows(first, n, rq), :] for sh in (second, third)]
+        parts += [gr_ref.at[sh, rows(first, n, ro), :] for sh in near_shard]
         waves_q.append([cp.make(part, part, (dev, m)) for part in parts])
+    rf = (gr_ref.shape[1] - n_out) // 8
     waves_r = []
-    wide = gr_ref.shape[2] // FORWARD_CHUNKS
-    for c in range(FORWARD_CHUNKS):
-        cols = pl.ds(c * wide, wide)
-        part = gr_ref.at[m, rows(piece, 1, rr), cols]
-        ws = [[cp.make(part, part, (d, o)) for o in others]]
+    for u in range(3):
+        part = gr_ref.at[m, pl.ds(pl.multiple_of(n_out + piece * rf, 16), rf), :]
+        ws = [[cp.make(part, part, (d, far[u]))]]
         for dev, first, n in steps:
-            parts = [gr_ref.at[sh, rows(first, n, rr), cols] for sh in froms]
-            ws.append([cp.make(part, part, (dev, m)) for part in parts])
+            part = gr_ref.at[near_shard[u], pl.ds(pl.multiple_of(n_out + first * rf, 16), n * rf), :]
+            ws.append([cp.make(part, part, (dev, m))])
         waves_r.append(ws)
 
     def pass_on(waves, st):
@@ -182,10 +188,11 @@
     def token_copy(k, i):
         ls, n, slot, fs, other = SEGMENTS[k][i]
         return pltpu.make_async_remote_copy(
-            x_ref.at[pl.ds(ls, n), :], tok.at[slot, pl.ds(fs, n), :],
+            x_hbm.at[pl.ds(ls, n), :], tok.at[slot, pl.ds(fs, n), :],
             tsend.at[i], trecv.at[slot], device_id=(d, other), device_id_type=MESH)
 
-    barrier([(d, o) for o in others] + [(o, m) for o in plane] + [(h, m) for h in highs])
+    pl.semaphore_wait(entry, len(partners))
+    own[0].wait()
     start(waves_q[0])
     for k in range(4):
         @pl.when(m == k)
@@ -208,6 +215,7 @@
 
         lax.fori_loop(0, n // 256, block, 0)
 
+    x_copy.wait()
     for k in range(4):
         @pl.when(m == k)
         def _():
@@ -245,6 +253,8 @@
 
     pass_on(waves_q, 1)
     remote_rows((0, 1, 1, 0))
+    own[1].wait()
+    own[2].wait()
     for ws in waves_r:
         start(ws[0])
 
@@ -253,9 +263,12 @@
         (0, 2): lambda: pass_on(waves_q, 3),
         (0, 4): lambda: pass_on(waves_r[0], 1),
         (1, 1): lambda: pass_on(waves_r[1], 1),
-        (1, 3): lambda: pass_on(waves_r[0], 2),
-        (2, 1): lambda: pass_on(waves_r[1], 2),
-        (2, 3): lambda: pass_on(waves_r[0], 3),
+        (1, 2): lambda: pass_on(waves_r[0], 2),
+        (1, 4): lambda: pass_on(waves_r[2], 1),
+        (2, 0): lambda: pass_on(waves_r[1], 2),
+        (2, 1): lambda: pass_on(waves_r[0], 3),
+        (2, 2): lambda: pass_on(waves_r[2], 2),
+        (2, 4): lambda: pass_on(waves_r[1], 3),
     }
 
     def task(t, carry):
@@ -322,11 +335,12 @@
         return carry
 
     lax.fori_loop(0, 3, task, 0)
-    for ws in waves_r[1:]:
-        pass_on(ws, 3)
+    pass_on(waves_r[2], 3)
+    arrive(waves_q[3][2:])
     for h in range(2):
         spill(2, h).wait()
     n_rows = x_ref.shape[0]
+    cot_copy.wait()
     row = m * n_rows + lax.broadcasted_iota(jnp.int32, (n_rows, 1), 0)
     mask = (row // PATCH < live_ref[0]).astype(F32)
     gf_sc = p_sc.at[1, pl.ds(0, n_rows), pl.ds(512, 512)]
@@ -347,8 +361,6 @@
                             device_id=(d, other), device_id_type=MESH).wait_recv()
             for t in range(3):
                 keep_copy(k, t).wait()
-    for ws in waves_r:
-        arrive(ws[3])
 
 
     wo = jnp.concatenate([gr_ref[s, 0:PAIR, :] for s in range(4)], axis=0)
@@ -422,12 +434,18 @@
             double_u[i + 1].start()
 
     hidden_schedule = {
-        2: lambda: flows[0].run(1),
-        3: lambda: (flows[0].run(2), flows[1].run(1)),
+        1: lambda: (flows[0].run(1),),
+        2: lambda: (flows[1].run(1),),
+        3: lambda: (flows[0].run(2), flows[2].run(1),),
     }
 
     def hidden(i, carry):
         s = (m + 1 + i) % 4
+        for u in range(3):
+            @pl.when(i == u)
+            def _():
+                arrive(waves_r[u][3])
+
         up = gr_ref[s, PAIR:PAIR + 512, :]
         down = gr_ref[s, PAIR + 512:, :]
         pre = nn_dot(e2_in[...], up) + gb_ref[s, 1:2, :]
@@ -598,9 +616,7 @@
 
     early, late = Small(0), Small(1)
 
-    flows[0].run(3)
     flows[1].run(2)
-    flows[2].run(1)
     gw = tn_dot(mix, ga).astype(BF16)
     for s in range(4):
         dw_sc[s] = gw[s * PAIR:(s + 1) * PAIR, :]
@@ -610,8 +626,10 @@
     os_ref[2:3, :] = jnp.sum(ga.astype(F32), axis=0, keepdims=True)
     early.run(0)
     out_ref[...] = (mask * (res_sc[...] + pn_sc[0, 0:n_rows, :] + vec_ref[5:6, :])).astype(BF16)
+    out_copy_back = pltpu.make_async_copy(out_ref, out_hbm, outsem)
+    out_copy_back.start()
     res_sc[...] = gres
-    flows[1].run(3)
+    flows[0].run(3)
     flows[2].run(2)
     flows[3].run(1)
 
@@ -661,15 +679,15 @@
         os_ref[9:10, :] += bias_sum
 
     back_schedule = {
-        (0, 0): lambda: (flows[2].run(3), flows[3].run(2), outs.run(1)),
-        (0, 1): lambda: (flows[3].run(3), early.run(1)),
-        (0, 2): lambda: outs.run(2),
-        (1, 0): lambda: combine_u(),
-        (1, 1): lambda: (heads[2].run(1), early.run(2), more_u(0)),
-        (1, 2): lambda: (heads[2].run(2), combine_w()),
-        (2, 0): lambda: more_u(1),
-        (2, 1): lambda: (heads[0].run(1), spread_w.run(1)),
-        (2, 2): lambda: (heads[0].run(2), more_u(2)),
+        (0, 0): lambda: (flows[1].run(3),),
+        (0, 1): lambda: (flows[3].run(2), flows[2].run(3), early.run(1), outs.run(1),),
+        (0, 2): lambda: (flows[3].run(3), outs.run(2),),
+        (1, 0): lambda: (combine_u(),),
+        (1, 1): lambda: (heads[2].run(1), early.run(2), more_u(0),),
+        (1, 2): lambda: (heads[2].run(2), combine_w(),),
+        (2, 0): lambda: (more_u(1),),
+        (2, 1): lambda: (heads[0].run(1), spread_w.run(1),),
+        (2, 2): lambda: (heads[0].run(2), more_u(2),),
     }
     width = 256
 
@@ -710,6 +728,8 @@
         k = qkv_ref[t, :, PAIR:2 * PAIR]
         v = qkv_ref[t, :, 2 * PAIR:]
         zero = jnp.zeros_like(k)
+        dop = scaled.astype(BF16).astype(F32).T.astype(BF16)
+        kt = k.astype(F32).T.astype(BF16)
         dqt = []
         for h in range(2):
             fetch(t, h).wait()
@@ -717,13 +737,11 @@
             part = slice(h * HEAD, (h + 1) * HEAD)
             vm = jnp.where(sel, v, zero)
             center = jnp.sum(qt_sc[part, :].astype(F32) * ot_ref[t, part, :], axis=0, keepdims=True)
-            dop = qt_sc[...].astype(F32).T.astype(BF16)
             dv = nn_dot(p_sc[h], jnp.where(sel, dop, zero))
             for c in range(PATCH // width):
                 cols = slice(c * width, (c + 1) * width)
                 dpt = nn_dot(vm, qt_sc[:, cols])
                 p_sc[h, :, cols] = (p_sc[h, :, cols].astype(F32) * (dpt - center[:, cols])).astype(BF16)
-            kt = k.astype(F32).T.astype(BF16)
             dqt.append(nn_dot(kt[part], p_sc[h]))
             dk = nn_dot(p_sc[h], jnp.where(sel, qs, zero))
 
@@ -793,7 +811,6 @@
     oq_ref[rows(piece, 1, rq), :] = acc.astype(BF16)
     spread_q.run(0)
 
-    spread_q.run(1)
     for k in range(4):
         @pl.when(m == k)
         def _():
@@ -802,6 +819,8 @@
                 pltpu.make_async_remote_copy(part, part, bsend.at[i], brecv.at[slot],
                                              device_id=(d, other), device_id_type=MESH).wait_recv()
     for r in range(0, n_rows, 256):
+        if r == 512:
+            spread_q.run(1)
         rs = slice(r, r + 256)
         gn = xhat_sc[rs, :] + got_sc[rs, :].astype(F32)
         xhat = xn_sc[rs, :].astype(F32)
@@ -822,6 +841,7 @@
                 row_copy(k, i).wait_send()
             for c in head_copies(k):
                 c.wait_send()
+    out_copy_back.wait()
     cp.finish()
 
 
@@ -832,7 +852,7 @@
     rows_o = wo.shape[0]
     rq, ro, ru = wq.shape[0] // 8, rows_o // 8, rows_u // 8
     high = max(n_high, 1)
-    copies = 11 + FORWARD_CHUNKS * 12 + 18 + 14 + 7 + 20 + 8 + 5 * n_high
+    copies = 3 + 20 + 12 + 18 + 14 + 7 + 20 + 8 + 5 * n_high
     vmem = pl.BlockSpec(memory_space=pltpu.VMEM)
     ve = pltpu.VMEM
     return pl.pallas_call(
@@ -847,10 +867,10 @@
             jax.ShapeDtypeStruct((16, 512), F32),
             jax.ShapeDtypeStruct((3, 2, PATCH, PATCH), BF16),
         ),
-        in_specs=[pl.BlockSpec(memory_space=pltpu.SMEM)] + [vmem] * 15,
-        out_specs=(vmem,) * 6 + (ANY,),
+        in_specs=[pl.BlockSpec(memory_space=pltpu.SMEM), ANY, ANY] + [vmem] * 3 + [ANY] * 3 + [vmem] * 7,
+        out_specs=(ANY,) + (vmem,) * 5 + (ANY,),
         scratch_shapes=[
-            ve((16, 512), F32),
+            ve((n, 512), BF16), ve((n, 512), BF16), ve((n, 512), BF16), ve((16, 512), F32),
             ve((2, PATCH, 512), BF16), ve((2, PATCH, 512), BF16), ve((4, 8 * rq, cols_q), BF16),
             ve((4, rows_o + rows_u, 512), BF16), ve((4, 8, 512), F32), ve((3, PATCH, cols_q), BF16),
             ve((3, 8, PATCH), F32), ve((3, PAIR, PATCH), F32), ve((4, n, PAIR), BF16), ve((2, PATCH, PAIR), BF16),
@@ -865,7 +885,7 @@
             ve((4, 4 * ru, 512), BF16), ve((4, 2 * ru, 512), BF16), ve((4, ru, 512), BF16), ve((3, ru, 512), BF16),
             ve((high, ru, 512), BF16), ve((high, rq, cols_q), BF16), ve((high, ro, 512), BF16),
             ve((2, 8, 8, 512), F32), ve((2, 4, 8, 512), F32), ve((2, high + 1, 8, 512), F32),
-            dma((2,)), dma((3,)), dma((copies,)), dma((copies,)), dma((2,)), dma((2,)), dma((3,)), dma((2, 4)),
+            dma((2,)), dma((3,)), dma((2,)), dma((3,)), dma, dma((copies,)), dma((copies,)), dma((2,)), dma((2,)), dma((3,)), dma((2, 4)),
             dma((5,)), dma((3,)), dma((2,)), dma((2,)),
         ],
         compiler_params=pltpu.CompilerParams(collective_id=0, has_side_effects=True, vmem_limit_bytes=VMEM_LIMIT),
@@ -892,7 +912,7 @@
 
 
 def unpack(pick, out, gt, q, o, u, s):
-    steps = 4
+    steps = 2
     n, rq, ro, ru = out.shape[0] // steps, q.shape[0] // steps, o.shape[0] // steps, u.shape[0] // (2 * steps)
 
     def block(r, c):

time: 146 us -> 137 us (0.938)
  Pallas kernels: 143 us -> 133 us
    pallas_call x1, Pallas kernels: 139 us -> 129 us  [layer(): pl.pallas_call(functools.partial(layer_kernel, n_high), name='layer', out...]
where the time goes in v4:
time: 137 us; the launch traced here: 136 us
  Pallas kernels  133 us (97%)
  between operations  1.49 us (1%)
    pallas_call x1, Pallas kernels, layer(): pl.pallas_call(functools.partial(layer_kernel, n_high), name='layer', out...  129 us
    pallas_call x1, Pallas kernels, unpack(): pl.pallas_call(unpack_kernel, name='unpack', grid=(steps,), out_shape=(ja...  3.87 us

profile of v4, /device:TPU:1, one launch (start us, length us, event | category | flops | bytes accessed | tf_op | source)
XLA Modules:
  0.0 135.7 jit_solution(12288100009128090857)
XLA Ops:
  0.7 0.7 pad_maximum_fusion
  1.4 0.6 reshape.92.b3
  2.6 129.0 %layer.1 = (bf16[768,512]{1,0:T(8,128)(2,1)}, bf16[768,512]{1,0:T(8,128)(2,1)}, bf16[512,384]{1,0:T(8,128)(2,1)}, bf16[128,512]{1,0:T(8,128)(2,1)}, bf16[1024,51...) custom-call(s32[1]{0:T(128)S(6)} %copy.35.live_ref, bf16[768,512]{1,0:T(8,128)(2,1)} %x_hbm.1, ...), custom_call_target="tpu_custom_call" | custom-call | tf_op jit(solution)/shard_map/layer/pallas_call | solution.py:858
  131.6 3.9 %unpack.1 = (bf16[768,512]{1,0:T(8,128)(2,1)}, bf16[768,512]{1,0:T(8,128)(2,1)}, f32[512,128]{1,0:T(8,128)}, f32[512,128]{1,0:T(8,128)}, f32[512,128]{1,0:T(8,12...) custom-call(s32[1]{0:T(128)} %bitcast.pick_ref, ...), custom_call_target="tpu_custom_call" | custom-call | tf_op jit(solution)/shard_map/unpack/pallas_call | solution.py:925

commit v5 on v4

--- a/solution.py
+++ b/solution.py
@@ -617,6 +617,7 @@
     early, late = Small(0), Small(1)
 
     flows[1].run(2)
+    flows[3].run(1)
     gw = tn_dot(mix, ga).astype(BF16)
     for s in range(4):
         dw_sc[s] = gw[s * PAIR:(s + 1) * PAIR, :]
@@ -631,7 +632,6 @@
     res_sc[...] = gres
     flows[0].run(3)
     flows[2].run(2)
-    flows[3].run(1)
 
     def first_stats(i, carry):
         rs = pl.ds(pl.multiple_of(i * 256, 256), 256)
@@ -679,8 +679,8 @@
         os_ref[9:10, :] += bias_sum
 
     back_schedule = {
-        (0, 0): lambda: (flows[1].run(3),),
-        (0, 1): lambda: (flows[3].run(2), flows[2].run(3), early.run(1), outs.run(1),),
+        (0, 0): lambda: (flows[1].run(3), flows[3].run(2),),
+        (0, 1): lambda: (flows[2].run(3), early.run(1), outs.run(1),),
         (0, 2): lambda: (flows[3].run(3), outs.run(2),),
         (1, 0): lambda: (combine_u(),),
         (1, 1): lambda: (heads[2].run(1), early.run(2), more_u(0),),

time: 137 us -> 136 us (level); the launches traced: 136 us -> 136 us
  no operation moved by 1% of the time
where the time goes in v5:
time: 136 us
  Pallas kernels  133 us (98%)
  between operations  1.49 us (1%)
    pallas_call x1, Pallas kernels, layer(): pl.pallas_call(functools.partial(layer_kernel, n_high), name='layer', out...  129 us
    pallas_call x1, Pallas kernels, unpack(): pl.pallas_call(unpack_kernel, name='unpack', grid=(steps,), out_shape=(ja...  3.87 us

profile of v5, /device:TPU:1, one launch (start us, length us, event | category | flops | bytes accessed | tf_op | source)
XLA Modules:
  0.0 136.1 jit_solution(1439518607492401497)
XLA Ops:
  0.7 0.7 pad_maximum_fusion
  1.4 0.6 reshape.92.b3
  2.6 129.4 %layer.1 = (bf16[768,512]{1,0:T(8,128)(2,1)}, bf16[768,512]{1,0:T(8,128)(2,1)}, bf16[512,384]{1,0:T(8,128)(2,1)}, bf16[128,512]{1,0:T(8,128)(2,1)}, bf16[1024,51...) custom-call(s32[1]{0:T(128)S(6)} %copy.35.live_ref, bf16[768,512]{1,0:T(8,128)(2,1)} %x_hbm.1, ...), custom_call_target="tpu_custom_call" | custom-call | tf_op jit(solution)/shard_map/layer/pallas_call | solution.py:858
  132.0 3.9 %unpack.1 = (bf16[768,512]{1,0:T(8,128)(2,1)}, bf16[768,512]{1,0:T(8,128)(2,1)}, f32[512,128]{1,0:T(8,128)}, f32[512,128]{1,0:T(8,128)}, f32[512,128]{1,0:T(8,12...) custom-call(s32[1]{0:T(128)} %bitcast.pick_ref, ...), custom_call_target="tpu_custom_call" | custom-call | tf_op jit(solution)/shard_map/unpack/pallas_call | solution.py:925

commit v6 on v5

--- a/solution.py
+++ b/solution.py
@@ -790,16 +790,16 @@
         return carry
 
     lax.fori_loop(0, 3, back_task, 0)
+    heads[1].run(1)
     late.run(0)
-    heads[1].run(1)
     xn_sc = p_sc.at[0, pl.ds(0, n_rows), pl.ds(0, 512)]
     for k in range(4):
         @pl.when(m == k)
         def _():
             for ls, n, slot, fs, other in SEGMENTS[k]:
                 xn_sc[ls:ls + n, :] = tok[slot, fs:fs + n, :]
+    heads[1].run(2)
     late.run(1)
-    heads[1].run(2)
     acc = dq_sc[0, rows(piece, 1, rq), :].astype(F32)
     for t in (2, 1):
         heads[t].across[0].wait_recv()

time: 136 us -> 136 us (level)
  no operation moved by 1% of the time
where the time goes in v6:
time: 136 us; the launch traced here: 135 us
  Pallas kernels  133 us (98%)
  between operations  1.49 us (1%)
    pallas_call x1, Pallas kernels, layer(): pl.pallas_call(functools.partial(layer_kernel, n_high), name='layer', out...  129 us
    pallas_call x1, Pallas kernels, unpack(): pl.pallas_call(unpack_kernel, name='unpack', grid=(steps,), out_shape=(ja...  3.87 us

profile of v6, /device:TPU:1, one launch (start us, length us, event | category | flops | bytes accessed | tf_op | source)
XLA Modules:
  0.0 135.3 jit_solution(1688549299554920352)
XLA Ops:
  0.7 0.7 pad_maximum_fusion
  1.4 0.6 reshape.92.b3
  2.6 128.6 %layer.1 = (bf16[768,512]{1,0:T(8,128)(2,1)}, bf16[768,512]{1,0:T(8,128)(2,1)}, bf16[512,384]{1,0:T(8,128)(2,1)}, bf16[128,512]{1,0:T(8,128)(2,1)}, bf16[1024,51...) custom-call(s32[1]{0:T(128)S(6)} %copy.35.live_ref, bf16[768,512]{1,0:T(8,128)(2,1)} %x_hbm.1, ...), custom_call_target="tpu_custom_call" | custom-call | tf_op jit(solution)/shard_map/layer/pallas_call | solution.py:858
  131.3 3.9 %unpack.1 = (bf16[768,512]{1,0:T(8,128)(2,1)}, bf16[768,512]{1,0:T(8,128)(2,1)}, f32[512,128]{1,0:T(8,128)}, f32[512,128]{1,0:T(8,128)}, f32[512,128]{1,0:T(8,12...) custom-call(s32[1]{0:T(128)} %bitcast.pick_ref, ...), custom_call_target="tpu_custom_call" | custom-call | tf_op jit(solution)/shard_map/unpack/pallas_call | solution.py:925
